TPU v7x, 256 devices: a whole 4x4x8 slice. The times are simulated.
256 devices in a mesh: rep: 8 (over y, x_hi), blk: 32 (over z, x_lo, core).
Axes of the slice: x: 4 (x_hi: 2, x_lo: 2; x = x_hi * 2 + x_lo), y: 4, z: 8, core: 2. Of those that a mesh axis runs over, the one named last changes fastest.
Arguments:
- features: bfloat16 [131072, 128], P(('rep', 'blk')), may hold values from -6 to 6
- degrees: int32 [131072], P(('rep', 'blk')), may hold values from 1 to 32
- tile_weights: bfloat16 [8, 32, 320, 128, 128], P('rep', 'blk'), may hold values from 0 to 0.049804688
- tile_rows: int32 [8, 32, 320], P('rep', 'blk'), may hold values from 0 to 127, as said below
- tile_cols: int32 [8, 32, 320], P('rep', 'blk'), may hold values from 0 to 31, as said below
- tile_counts: int32 [8, 32], P('rep', 'blk'), may hold values from 1 to 320, as said below
- weight: bfloat16 [128, 256], replicated, may hold values from -0.5 to 0.5
- layer_bias: float32 [256], replicated, may hold values from -3 to 3
- upstream: bfloat16 [131072, 256], P(('rep', 'blk')), may hold values from -6 to 6
Outputs:
- hidden: bfloat16 [131072, 256], P(('rep', 'blk'))
- feature_grad: bfloat16 [131072, 128], P(('rep', 'blk'))
- weight_grad: float32 [128, 256], replicated
- bias_grad: float32 [256], replicated
Inputs may be any that keep to these rules, and one draw needn't show every extreme that they name: `tile_rows`: the first tile_counts slots of a device hold distinct tiles, ordered by row and then by column; a used row h lies in node block r * 32 + h // 4, whose index h // 4 is within 3 steps of the device's blk index around the loop of 32; unused slots hold the device's own first tile row. `tile_cols`: unused slots hold 0. `tile_counts`: at most 80 used slots of one device lie in the rows of one node block; this and the largest count are both reached by some device in every draw.
All inputs are finite; a program needn't handle non-finite values.
Results may differ from a plain program's by a relative error of at most 0.015.
Values may be sent and summed in bfloat16 or wider, within the bound.
A program may use at most 128 MiB of HBM per device.

v0:
```python
import jax
import jax.numpy as jnp
from jax import lax
from jax.sharding import PartitionSpec as P

REACH = 3


def shifted(value, axis, by):
    length = lax.axis_size(axis)
    return lax.ppermute(value, axis, [(i, (i + by) % length) for i in range(length)])


def node_scale(degrees):
    return 1.0 / jnp.sqrt(degrees.astype(jnp.float32) + 1.0)


def on_device(
    features, degrees, tile_weights, tile_rows, tile_cols, tile_counts, weight, layer_bias, upstream
):
    row_count, feat_width = features.shape
    tile_size = tile_weights.shape[-1]
    slot_total = tile_weights.shape[2]
    row_tiles = row_count // tile_size
    rep_count = lax.axis_size("rep")
    blk_count = lax.axis_size("blk")
    blk_index = lax.axis_index("blk")
    window_blocks = 2 * REACH + 1
    window_tiles = window_blocks * row_tiles
    column_tiles = rep_count * row_tiles
    slot_block = slot_total // (2 * (REACH + 1))
    block_total = slot_total // slot_block
    weights_dev = tile_weights[0, 0]
    rows_dev = tile_rows[0, 0]
    cols_dev = tile_cols[0, 0]
    count_dev = tile_counts[0, 0]
    group_index = rows_dev // row_tiles
    distance = (group_index - blk_index) % blk_count
    distance = jnp.where(distance > blk_count // 2, distance - blk_count, distance)
    window_rows = (distance + REACH) * row_tiles + rows_dev % row_tiles
    slot_ids = jnp.arange(slot_total, dtype=jnp.int32)
    slot_valid = slot_ids < count_dev
    window_seg = jnp.where(slot_valid, window_rows, window_tiles)
    column_seg = jnp.where(slot_valid, cols_dev, column_tiles)

    def tile_pass(source_tiles, gather_index, segment_index, segment_total, pattern):

        def add_block(block_id, running):
            slot_first = block_id * slot_block
            weights_part = lax.dynamic_slice_in_dim(weights_dev, slot_first, slot_block, 0)
            gather_part = lax.dynamic_slice_in_dim(gather_index, slot_first, slot_block, 0)
            segment_part = lax.dynamic_slice_in_dim(segment_index, slot_first, slot_block, 0)
            products = jnp.einsum(
                pattern, weights_part, source_tiles[gather_part], preferred_element_type=jnp.float32
            )
            return (
                running
                + jax.ops.segment_sum(products, segment_part, segment_total + 1)[:segment_total]
            )

        zero_sum = jnp.zeros((segment_total, tile_size, feat_width), jnp.float32)
        return lax.fori_loop(0, block_total, add_block, zero_sum)

    node_norm = node_scale(degrees)
    scaled = (node_norm[:, None] * features.astype(jnp.float32)).astype(jnp.bfloat16)
    source_rows = lax.all_gather(scaled, "rep", axis=0, tiled=True)
    source_tiles = source_rows.reshape(column_tiles, tile_size, feat_width)
    partial_value = tile_pass(source_tiles, cols_dev, window_seg, window_tiles, "tab,tbf->taf")
    partial_value = partial_value.reshape(window_blocks, row_count, feat_width)
    neighbor_sum = partial_value[REACH]
    for offset in range(-REACH, REACH + 1):
        if offset != 0:
            neighbor_sum = neighbor_sum + shifted(
                partial_value[offset + REACH].astype(jnp.bfloat16), "blk", offset
            ).astype(jnp.float32)
    aggregated = (node_norm[:, None] * (neighbor_sum + scaled.astype(jnp.float32))).astype(
        jnp.bfloat16
    )
    pre_act = jnp.dot(aggregated, weight, preferred_element_type=jnp.float32) + layer_bias
    hidden = jax.nn.silu(pre_act).astype(jnp.bfloat16)
    gate_sigmoid = jax.nn.sigmoid(pre_act)
    pre_grad = (
        upstream.astype(jnp.float32)
        * (gate_sigmoid + pre_act * gate_sigmoid * (1.0 - gate_sigmoid))
    ).astype(jnp.bfloat16)
    local_weight = jnp.dot(aggregated.T, pre_grad, preferred_element_type=jnp.float32)
    local_bias = jnp.sum(pre_grad.astype(jnp.float32), axis=0)
    weight_sum, bias_sum = lax.psum((local_weight, local_bias), ("rep", "blk"))
    grad_scale = (row_count * rep_count * blk_count) ** (-0.5)
    scaled_grad = (
        node_norm[:, None] * jnp.dot(pre_grad, weight.T, preferred_element_type=jnp.float32)
    ).astype(jnp.bfloat16)
    window_parts = [scaled_grad] * window_blocks
    for offset in range(-REACH, REACH + 1):
        if offset != 0:
            window_parts[offset + REACH] = shifted(scaled_grad, "blk", -offset)
    grad_tiles = jnp.stack(window_parts).reshape(window_tiles, tile_size, feat_width)
    column_part = tile_pass(grad_tiles, window_rows, column_seg, column_tiles, "tab,taf->tbf")
    column_sum = lax.psum_scatter(
        column_part.reshape(rep_count * row_count, feat_width).astype(jnp.bfloat16),
        "rep",
        scatter_dimension=0,
        tiled=True,
    ).astype(jnp.float32)
    feature_grad = (node_norm[:, None] * (column_sum + scaled_grad.astype(jnp.float32))).astype(
        jnp.bfloat16
    )
    return (hidden, feature_grad, weight_sum * grad_scale, bias_sum * grad_scale)


def solution(mesh):
    placed = (
        P(("rep", "blk"), None),
        P(("rep", "blk")),
        P("rep", "blk", None, None, None),
        P("rep", "blk", None),
        P("rep", "blk", None),
        P("rep", "blk"),
        P(),
        P(),
        P(("rep", "blk"), None),
    )
    return jax.shard_map(
        on_device,
        mesh=mesh,
        in_specs=placed,
        out_specs=(P(("rep", "blk"), None), P(("rep", "blk"), None), P(), P()),
        check_vma=False,
    )
```

profile of v0, /device:TPU:32, one launch (start us, length us, event | category | flops | bytes accessed | tf_op | source)
XLA Modules:
  0.0 557.3 jit_solution(4385618830677992955)
XLA Ops:
  11.8 53.4 %all-gather.2.cloned.1.call-done = bf16[4096,128]{1,0:T(8,128)(2,1)} async-done(((bf16[512,128]{1,0:T(8,128)(2,1)}), bf16[4096,128]{1,0:T(8,128)(2,1)}) %all-gather.2.cloned.1.call-update) | async-done | bytes 1048592 | tf_op jit(solution)/shard_map/all_gather | solution.py:66
  65.2 120.5 %while.28 = (s32[]{:T(128)}, f32[28,128,128]{2,1,0:T(8,128)}, s32[320]{0:T(512)S(1)}, bf16[320,128,128]{2,1,0:T(8,128)(2,1)}, s32[320]{0:T(512)S(1)}, /*index=5*...) while((s32[]{:T(128)}, f32[28,128,128]{2,1,0:T(8,128)}, ...), condition=%wide.region_2.3_spmd.clone, body=%wide.region_0.2_spmd.clone.sunk | while | flops 169346176 | bytes 23139612 | solution.py:62
  67.4 3.3 fusion.44
  71.0 6.5 %scatter_fusion = f32[29,128,128]{2,1,0:T(8,128)S(1)} fusion(f32[29,128,128]{2,1,0:T(8,128)S(1)} %broadcast.127, s32[40]{0:T(128)S(1)} %dynamic_slice.62, f32[40,128,128]{2,1,0:T(8,128)} %fusion.44), kind=kCustom, calls=%fused_computation.2.clone.clone.1 | custom fusion | flops 655360 | bytes 7864480 | tf_op jit(solution)/shard_map/while/body/eval_jaxpr/scatter-add | solution.py:58
  84.7 6.5 %scatter_fusion = f32[29,128,128]{2,1,0:T(8,128)S(1)} fusion(f32[29,128,128]{2,1,0:T(8,128)S(1)} %broadcast.127, s32[40]{0:T(128)S(1)} %dynamic_slice.62, f32[40,128,128]{2,1,0:T(8,128)} %fusion.44), kind=kCustom, calls=%fused_computation.2.clone.clone.1 | custom fusion | flops 655360 | bytes 7864480 | tf_op jit(solution)/shard_map/while/body/eval_jaxpr/scatter-add | solution.py:58
  96.4 3.3 fusion.44
  100.0 6.5 %scatter_fusion = f32[29,128,128]{2,1,0:T(8,128)S(1)} fusion(f32[29,128,128]{2,1,0:T(8,128)S(1)} %broadcast.127, s32[40]{0:T(128)S(1)} %dynamic_slice.62, f32[40,128,128]{2,1,0:T(8,128)} %fusion.44), kind=kCustom, calls=%fused_computation.2.clone.clone.1 | custom fusion | flops 655360 | bytes 7864480 | tf_op jit(solution)/shard_map/while/body/eval_jaxpr/scatter-add | solution.py:58
  111.6 3.3 fusion.44
  115.2 6.5 %scatter_fusion = f32[29,128,128]{2,1,0:T(8,128)S(1)} fusion(f32[29,128,128]{2,1,0:T(8,128)S(1)} %broadcast.127, s32[40]{0:T(128)S(1)} %dynamic_slice.62, f32[40,128,128]{2,1,0:T(8,128)} %fusion.44), kind=kCustom, calls=%fused_computation.2.clone.clone.1 | custom fusion | flops 655360 | bytes 7864480 | tf_op jit(solution)/shard_map/while/body/eval_jaxpr/scatter-add | solution.py:58
  130.4 6.5 %scatter_fusion = f32[29,128,128]{2,1,0:T(8,128)S(1)} fusion(f32[29,128,128]{2,1,0:T(8,128)S(1)} %broadcast.127, s32[40]{0:T(128)S(1)} %dynamic_slice.62, f32[40,128,128]{2,1,0:T(8,128)} %fusion.44), kind=kCustom, calls=%fused_computation.2.clone.clone.1 | custom fusion | flops 655360 | bytes 7864480 | tf_op jit(solution)/shard_map/while/body/eval_jaxpr/scatter-add | solution.py:58
  145.7 6.5 %scatter_fusion = f32[29,128,128]{2,1,0:T(8,128)S(1)} fusion(f32[29,128,128]{2,1,0:T(8,128)S(1)} %broadcast.127, s32[40]{0:T(128)S(1)} %dynamic_slice.62, f32[40,128,128]{2,1,0:T(8,128)} %fusion.44), kind=kCustom, calls=%fused_computation.2.clone.clone.1 | custom fusion | flops 655360 | bytes 7864480 | tf_op jit(solution)/shard_map/while/body/eval_jaxpr/scatter-add | solution.py:58
  157.4 3.3 fusion.44
  160.9 6.5 %scatter_fusion = f32[29,128,128]{2,1,0:T(8,128)S(1)} fusion(f32[29,128,128]{2,1,0:T(8,128)S(1)} %broadcast.127, s32[40]{0:T(128)S(1)} %dynamic_slice.62, f32[40,128,128]{2,1,0:T(8,128)} %fusion.44), kind=kCustom, calls=%fused_computation.2.clone.clone.1 | custom fusion | flops 655360 | bytes 7864480 | tf_op jit(solution)/shard_map/while/body/eval_jaxpr/scatter-add | solution.py:58
  172.6 3.3 fusion.44
  176.2 6.5 %scatter_fusion = f32[29,128,128]{2,1,0:T(8,128)S(1)} fusion(f32[29,128,128]{2,1,0:T(8,128)S(1)} %broadcast.127, s32[40]{0:T(128)S(1)} %dynamic_slice.62, f32[40,128,128]{2,1,0:T(8,128)} %fusion.44), kind=kCustom, calls=%fused_computation.2.clone.clone.1 | custom fusion | flops 655360 | bytes 7864480 | tf_op jit(solution)/shard_map/while/body/eval_jaxpr/scatter-add | solution.py:58
  187.5 14.4 %copy.13 = bf16[1,1,320,128,128]{3,4,2,1,0:T(8,128)(2,1)} copy(bf16[1,1,320,128,128]{4,3,2,1,0:T(8,128)(2,1)} %bitcast.61) | data formatting | bytes 20971520 | tf_op args[2]
  209.3 4.2 collective-permute-done.4
  223.9 5.1 collective-permute-done.6
  230.9 5.0 collective-permute-done.7
  236.2 113.0 %while.29 = (s32[]{:T(128)}, f32[32,128,128]{2,1,0:T(8,128)}, s32[320]{0:T(512)S(1)}, bf16[320,128,128]{1,2,0:T(8,128)(2,1)}, s32[320]{0:T(512)S(1)}, /*index=5*...) while((s32[]{:T(128)}, f32[32,128,128]{2,1,0:T(8,128)}, ...), condition=%wide.region_5.6_spmd.clone, body=%wide.region_3.5_spmd.clone.sunk | while | flops 169477248 | bytes 24188188 | solution.py:62
  240.8 6.6 %scatter_fusion.1 = f32[33,128,128]{2,1,0:T(8,128)S(1)} fusion(f32[33,128,128]{2,1,0:T(8,128)S(1)} %broadcast.134, s32[40]{0:T(128)S(1)} %dynamic_slice.65, f32[40,128,128]{2,1,0:T(8,128)} %fusion.47), kind=kCustom, calls=%fused_computation.3.clone.clone.1 | custom fusion | flops 655360 | bytes 7864480 | tf_op jit(solution)/shard_map/while/body/eval_jaxpr/scatter-add | solution.py:58
  253.5 6.6 %scatter_fusion.1 = f32[33,128,128]{2,1,0:T(8,128)S(1)} fusion(f32[33,128,128]{2,1,0:T(8,128)S(1)} %broadcast.134, s32[40]{0:T(128)S(1)} %dynamic_slice.65, f32[40,128,128]{2,1,0:T(8,128)} %fusion.47), kind=kCustom, calls=%fused_computation.3.clone.clone.1 | custom fusion | flops 655360 | bytes 7864480 | tf_op jit(solution)/shard_map/while/body/eval_jaxpr/scatter-add | solution.py:58
  267.8 6.6 %scatter_fusion.1 = f32[33,128,128]{2,1,0:T(8,128)S(1)} fusion(f32[33,128,128]{2,1,0:T(8,128)S(1)} %broadcast.134, s32[40]{0:T(128)S(1)} %dynamic_slice.65, f32[40,128,128]{2,1,0:T(8,128)} %fusion.47), kind=kCustom, calls=%fused_computation.3.clone.clone.1 | custom fusion | flops 655360 | bytes 7864480 | tf_op jit(solution)/shard_map/while/body/eval_jaxpr/scatter-add | solution.py:58
  278.6 3.3 fusion.47
  282.2 6.6 %scatter_fusion.1 = f32[33,128,128]{2,1,0:T(8,128)S(1)} fusion(f32[33,128,128]{2,1,0:T(8,128)S(1)} %broadcast.134, s32[40]{0:T(128)S(1)} %dynamic_slice.65, f32[40,128,128]{2,1,0:T(8,128)} %fusion.47), kind=kCustom, calls=%fused_computation.3.clone.clone.1 | custom fusion | flops 655360 | bytes 7864480 | tf_op jit(solution)/shard_map/while/body/eval_jaxpr/scatter-add | solution.py:58
  296.5 6.6 %scatter_fusion.1 = f32[33,128,128]{2,1,0:T(8,128)S(1)} fusion(f32[33,128,128]{2,1,0:T(8,128)S(1)} %broadcast.134, s32[40]{0:T(128)S(1)} %dynamic_slice.65, f32[40,128,128]{2,1,0:T(8,128)} %fusion.47), kind=kCustom, calls=%fused_computation.3.clone.clone.1 | custom fusion | flops 655360 | bytes 7864480 | tf_op jit(solution)/shard_map/while/body/eval_jaxpr/scatter-add | solution.py:58
  310.8 6.6 %scatter_fusion.1 = f32[33,128,128]{2,1,0:T(8,128)S(1)} fusion(f32[33,128,128]{2,1,0:T(8,128)S(1)} %broadcast.134, s32[40]{0:T(128)S(1)} %dynamic_slice.65, f32[40,128,128]{2,1,0:T(8,128)} %fusion.47), kind=kCustom, calls=%fused_computation.3.clone.clone.1 | custom fusion | flops 655360 | bytes 7864480 | tf_op jit(solution)/shard_map/while/body/eval_jaxpr/scatter-add | solution.py:58
  325.1 6.5 %scatter_fusion.1 = f32[33,128,128]{2,1,0:T(8,128)S(1)} fusion(f32[33,128,128]{2,1,0:T(8,128)S(1)} %broadcast.134, s32[40]{0:T(128)S(1)} %dynamic_slice.65, f32[40,128,128]{2,1,0:T(8,128)} %fusion.47), kind=kCustom, calls=%fused_computation.3.clone.clone.1 | custom fusion | flops 655360 | bytes 7864480 | tf_op jit(solution)/shard_map/while/body/eval_jaxpr/scatter-add | solution.py:58
  339.4 6.5 %scatter_fusion.1 = f32[33,128,128]{2,1,0:T(8,128)S(1)} fusion(f32[33,128,128]{2,1,0:T(8,128)S(1)} %broadcast.134, s32[40]{0:T(128)S(1)} %dynamic_slice.65, f32[40,128,128]{2,1,0:T(8,128)} %fusion.47), kind=kCustom, calls=%fused_computation.3.clone.clone.1 | custom fusion | flops 655360 | bytes 7864480 | tf_op jit(solution)/shard_map/while/body/eval_jaxpr/scatter-add | solution.py:58
  351.9 75.9 %psum.15 = f32[256]{0:T(256)S(1)} all-reduce(f32[256]{0:T(256)S(1)} %get-tuple-element.296), channel_id=1, replica_groups=mesh['rep'=8,'blk'=32] {'rep','blk'}, use_global_device_ids=true, to_apply=%region_9.10 | all-reduce | flops 256 | bytes 2048 | tf_op jit(solution)/shard_map/psum | solution.py:88
  428.4 41.2 %all-reduce.2.cloned.1.call-done = f32[128,256]{1,0:T(8,128)} async-done(((f32[128,256]{1,0:T(8,128)}), f32[128,256]{1,0:T(8,128)}) %all-reduce.2.cloned.1.call-update) | async-done | bytes 131088 | tf_op jit(solution)/shard_map/psum | solution.py:88
  471.1 77.9 %reduce-scatter.2.cloned.1.call-done = bf16[512,128]{1,0:T(8,128)(2,1)} async-done(((bf16[4096,128]{1,0:T(8,128)(2,1)}), bf16[512,128]{1,0:T(8,128)(2,1)}) %reduce-scatter.2.cloned.1.call-update) | async-done | bytes 131088 | tf_op jit(solution)/shard_map/reduce_scatter | solution.py:99
  (167 shorter events, 140.3 us)
Async XLA Ops:
  7.2 208.5 %copy-start = (bf16[128,256]{1,0:T(8,128)(2,1)S(1)}, bf16[128,256]{1,0:T(8,128)(2,1)}, u32[]{:S(2)}) copy-start(bf16[128,256]{1,0:T(8,128)(2,1)} %param.19) | copy-start | bytes 196612
  7.2 58.0 %all-gather.2.cloned.1.call-start = ((), (), s32[]{:S(2)}) async-start(), calls=%async_computation.1 | async-start | bytes 1179648 | tf_op jit(solution)/shard_map/all_gather | solution.py:66
  9.6 459.9 %all-reduce.2.cloned.1.call-start = ((), (), s32[]{:S(2)}) async-start(), calls=%async_computation.3 | async-start | bytes 262144 | tf_op jit(solution)/shard_map/psum | solution.py:88
  187.4 19.5 %collective-permute-start.5 = (bf16[512,128]{1,0:T(8,128)(2,1)S(1)}, bf16[512,128]{1,0:T(8,128)(2,1)S(1)}, u32[]{:S(2)}, u32[]{:S(2)}) collective-permute-start(bf16[512,128]{1,0:T(8,128)(2,1)S(1)} %bitcast.69), channel_id=1, source_target_pairs={{0,3},{1,4},{2,5},{3,6},{4,7},{5,8},{6,9},{7,10},{8,11},{9,12},{10... | collective-permute-start | bytes 393224 | tf_op jit(solution)/shard_map/ppermute | solution.py:11
  187.5 28.0 %copy-start.1 = (bf16[512,128]{1,0:T(8,128)(2,1)S(1)}, bf16[512,128]{1,0:T(8,128)(2,1)}, u32[]{:S(2)}) copy-start(bf16[512,128]{1,0:T(8,128)(2,1)} %param.13) | copy-start | bytes 393220
  187.5 28.2 %copy-start.2 = (bf16[512,256]{1,0:T(8,128)(2,1)S(1)}, bf16[512,256]{1,0:T(8,128)(2,1)}, u32[]{:S(2)}) copy-start(bf16[512,256]{1,0:T(8,128)(2,1)} %param.21) | copy-start | bytes 786436
  187.5 28.2 %copy-start.3 = (f32[256]{0:T(256)S(1)}, f32[256]{0:T(256)}, u32[]{:S(2)}) copy-start(f32[256]{0:T(256)} %param.20) | copy-start | bytes 3076
  202.0 7.3 %collective-permute-start = (bf16[512,128]{1,0:T(8,128)(2,1)S(1)}, bf16[512,128]{1,0:T(8,128)(2,1)S(1)}, u32[]{:S(2)}, u32[]{:S(2)}) collective-permute-start(bf16[512,128]{1,0:T(8,128)(2,1)S(1)} %bitcast.68), channel_id=1, source_target_pairs={{0,29},{1,30},{2,31},{3,0},{4,1},{5,2},{6,3},{7,4},{8,5},{9,6},{10... | collective-permute-start | bytes 393224 | tf_op jit(solution)/shard_map/ppermute | solution.py:11
  203.6 9.8 %collective-permute-start.4 = (bf16[512,128]{1,0:T(8,128)(2,1)S(1)}, bf16[512,128]{1,0:T(8,128)(2,1)S(1)}, u32[]{:S(2)}, u32[]{:S(2)}) collective-permute-start(bf16[512,128]{1,0:T(8,128)(2,1)S(1)} %bitcast.67), channel_id=1, source_target_pairs={{0,2},{1,3},{2,4},{3,5},{4,6},{5,7},{6,8},{7,9},{8,10},{9,11},{10,... | collective-permute-start | bytes 393224 | tf_op jit(solution)/shard_map/ppermute | solution.py:11
  204.2 9.3 %collective-permute-start.3 = (bf16[512,128]{1,0:T(8,128)(2,1)S(1)}, bf16[512,128]{1,0:T(8,128)(2,1)S(1)}, u32[]{:S(2)}, u32[]{:S(2)}) collective-permute-start(bf16[512,128]{1,0:T(8,128)(2,1)S(1)} %bitcast.66), channel_id=1, source_target_pairs={{0,1},{1,2},{2,3},{3,4},{4,5},{5,6},{6,7},{7,8},{8,9},{9,10},{10,1... | collective-permute-start | bytes 393224 | tf_op jit(solution)/shard_map/ppermute | solution.py:11
  204.2 9.3 %collective-permute-start.2 = (bf16[512,128]{1,0:T(8,128)(2,1)S(1)}, bf16[512,128]{1,0:T(8,128)(2,1)S(1)}, u32[]{:S(2)}, u32[]{:S(2)}) collective-permute-start(bf16[512,128]{1,0:T(8,128)(2,1)S(1)} %bitcast.65), channel_id=1, source_target_pairs={{0,31},{1,0},{2,1},{3,2},{4,3},{5,4},{6,5},{7,6},{8,7},{9,8},{10,9... | collective-permute-start | bytes 393224 | tf_op jit(solution)/shard_map/ppermute | solution.py:11
  206.9 8.6 %collective-permute-start.1 = (bf16[512,128]{1,0:T(8,128)(2,1)S(1)}, bf16[512,128]{1,0:T(8,128)(2,1)S(1)}, u32[]{:S(2)}, u32[]{:S(2)}) collective-permute-start(bf16[512,128]{1,0:T(8,128)(2,1)S(1)} %bitcast.64), channel_id=1, source_target_pairs={{0,30},{1,31},{2,0},{3,1},{4,2},{5,3},{6,4},{7,5},{8,6},{9,7},{10,... | collective-permute-start | bytes 393224 | tf_op jit(solution)/shard_map/ppermute | solution.py:11
  217.0 19.1 %collective-permute-start.11 = (bf16[512,128]{1,0:T(8,128)(2,1)S(1)}, bf16[512,128]{1,0:T(8,128)(2,1)S(1)}, u32[]{:S(2)}, u32[]{:S(2)}) collective-permute-start(bf16[512,128]{1,0:T(8,128)(2,1)S(1)} %fusion.6), channel_id=1, source_target_pairs={{0,29},{1,30},{2,31},{3,0},{4,1},{5,2},{6,3},{7,4},{8,5},{9,6},{10... | collective-permute-start | bytes 393224 | tf_op jit(solution)/shard_map/ppermute | solution.py:11
  217.9 18.2 %collective-permute-start.10 = (bf16[512,128]{1,0:T(8,128)(2,1)S(1)}, bf16[512,128]{1,0:T(8,128)(2,1)S(1)}, u32[]{:S(2)}, u32[]{:S(2)}) collective-permute-start(bf16[512,128]{1,0:T(8,128)(2,1)S(1)} %fusion.6), channel_id=1, source_target_pairs={{0,30},{1,31},{2,0},{3,1},{4,2},{5,3},{6,4},{7,5},{8,6},{9,7},{10,... | collective-permute-start | bytes 393224 | tf_op jit(solution)/shard_map/ppermute | solution.py:11
  219.0 17.1 %collective-permute-start.9 = (bf16[512,128]{1,0:T(8,128)(2,1)S(1)}, bf16[512,128]{1,0:T(8,128)(2,1)S(1)}, u32[]{:S(2)}, u32[]{:S(2)}) collective-permute-start(bf16[512,128]{1,0:T(8,128)(2,1)S(1)} %fusion.6), channel_id=1, source_target_pairs={{0,31},{1,0},{2,1},{3,2},{4,3},{5,4},{6,5},{7,6},{8,7},{9,8},{10,9... | collective-permute-start | bytes 393224 | tf_op jit(solution)/shard_map/ppermute | solution.py:11
  222.3 13.7 %collective-permute-start.8 = (bf16[512,128]{1,0:T(8,128)(2,1)S(1)}, bf16[512,128]{1,0:T(8,128)(2,1)S(1)}, u32[]{:S(2)}, u32[]{:S(2)}) collective-permute-start(bf16[512,128]{1,0:T(8,128)(2,1)S(1)} %fusion.6), channel_id=1, source_target_pairs={{0,1},{1,2},{2,3},{3,4},{4,5},{5,6},{6,7},{7,8},{8,9},{9,10},{10,1... | collective-permute-start | bytes 393224 | tf_op jit(solution)/shard_map/ppermute | solution.py:11
  222.3 6.7 %collective-permute-start.6 = (bf16[512,128]{1,0:T(8,128)(2,1)S(1)}, bf16[512,128]{1,0:T(8,128)(2,1)S(1)}, u32[]{:S(2)}, u32[]{:S(2)}) collective-permute-start(bf16[512,128]{1,0:T(8,128)(2,1)S(1)} %fusion.6), channel_id=1, source_target_pairs={{0,3},{1,4},{2,5},{3,6},{4,7},{5,8},{6,9},{7,10},{8,11},{9,12},{10... | collective-permute-start | bytes 393224 | tf_op jit(solution)/shard_map/ppermute | solution.py:11
  223.9 325.1 %reduce-scatter.2.cloned.1.call-start = ((), (), s32[]{:S(2)}) async-start(), calls=%async_computation.2 | async-start | bytes 1179648 | tf_op jit(solution)/shard_map/reduce_scatter | solution.py:99
  229.0 7.0 %collective-permute-start.7 = (bf16[512,128]{1,0:T(8,128)(2,1)S(1)}, bf16[512,128]{1,0:T(8,128)(2,1)S(1)}, u32[]{:S(2)}, u32[]{:S(2)}) collective-permute-start(bf16[512,128]{1,0:T(8,128)(2,1)S(1)} %fusion.6), channel_id=1, source_target_pairs={{0,2},{1,3},{2,4},{3,5},{4,6},{5,7},{6,8},{7,9},{8,10},{9,11},{10,... | collective-permute-start | bytes 393224 | tf_op jit(solution)/shard_map/ppermute | solution.py:11
Sparse Core Ops, SparseCore 0:
  11.2 53.9 all-gather.1
  224.0 245.4 all-reduce.1
  473.4 75.5 reduce-scatter.1
where the time goes:
time: 561 us; the launch traced here: 557 us
  waiting for transfers between devices  189 us (34%)
  other arithmetic  164 us (29%)
  blocking collectives  75.9 us (14%)
  matrix products  55.7 us (10%)
  local copies, waits for them, and re-layouts  42.9 us (8%)
  between operations  14.6 us (3%)
  starting transfers between devices  14.4 us (3%)
    scatter-add x16, other arithmetic, add_block(): jax.ops.segment_sum(products, segment_part, segment_total + 1)  105 us
    reduce_scatter x1, waiting for transfers between devices, on_device(): lax.psum_scatter(column_part.reshape(rep_count * row_count, feat_width).a...  77.9 us
    psum x1, blocking collectives, on_device(): weight_sum, bias_sum = lax.psum((local_weight, local_bias), ('rep', 'blk'))  75.9 us
    dot_general x16, matrix products, add_block(): jnp.einsum(pattern, weights_part, source_tiles[gather_part], preferred_el...  53.5 us
    all_gather x1, waiting for transfers between devices, on_device(): source_rows = lax.all_gather(scaled, 'rep', axis=0, tiled=True)  53.4 us
    add x16, other arithmetic, add_block(): running + jax.ops.segment_sum(products, segment_part, segment_total + 1)[...  46.3 us
    psum x1, waiting for transfers between devices, on_device(): weight_sum, bias_sum = lax.psum((local_weight, local_bias), ('rep', 'blk'))  41.2 us
    gather x16, local copies, waits for them, and re-layouts, add_block(): source_tiles[gather_part]  22.5 us
  transfers between devices with their start and end apart: 15, of which 7 were waited for; matrix products, arithmetic and copies ran while one was open for 24% of the time, Pallas kernels for 0%

commit v1 on v0

v1 whole, which is shorter than its diff:
```python
import itertools

import jax
import jax.numpy as jnp
from jax import lax
from jax.experimental import pallas as pl
from jax.experimental.pallas import tpu as pltpu
from jax.sharding import PartitionSpec as P

BF = jnp.bfloat16
F32 = jnp.float32
MESH = pl.DeviceIdType.MESH
SLOTS = 320
TS = 128
ROWS = 512
FEAT = 128
HID = 256
N_COPIES = 80
CHUNKS = 10
NODES = 131072


def kernel(
    rows_s,
    cols_s,
    count_s,
    feat_hbm,
    deg_ref,
    tiles_hbm,
    weight_ref,
    bias_ref,
    up_hbm,
    hidden_ref,
    fgrad_ref,
    wgrad_ref,
    bgrad_ref,
    feat_v,
    up_v,
    tile_v,
    tile_t,
    sums,
    xblk,
    xtransit,
    mate_out,
    mate_in,
    comb_out,
    comb_in,
    gblk,
    col_out,
    col_mid,
    col_in,
    xsum,
    xsum_transit,
    xsum_in,
    w_send,
    w_y,
    w_z,
    w_zin,
    w_x,
    w_xall,
    w_zall,
    w_all,
    table_v,
    table_s,
    local_sem,
    tile_sem,
    send_sem,
    recv_sem,
):
    rep = lax.axis_index("rep")
    blk = lax.axis_index("blk")
    y = lax.div(rep, 2)
    xh = lax.rem(rep, 2)
    z = lax.div(blk, 4)
    xl = lax.rem(lax.div(blk, 2), 2)
    core = lax.rem(blk, 2)
    y_plus = (lax.rem(rep + 2, 8), blk)
    y_minus = (lax.rem(rep + 6, 8), blk)
    blk_x = blk + 2 - 4 * xl
    x_plus = (2 * y + lax.rem(xh + xl, 2), blk_x)
    x_minus = (2 * y + lax.rem(xh + 1 - xl, 2), blk_x)
    mate = (rep, blk + 1 - 2 * core)
    k_plus = (rep, lax.rem(blk + 2, 32))
    k_minus = (rep, lax.rem(blk + 30, 32))
    single = (rep, lax.rem(blk + 29 + 6 * core, 32))
    y_peers = [(lax.rem(rep + 2 * j, 8), blk) for j in range(1, 4)]
    z_peers = [(rep, lax.rem(blk + 4 * j, 32)) for j in range(1, 8)]
    x_peers = [
        (
            2 * y + lax.rem(xh + j // 4, 2),
            4 * z + 2 * lax.rem(xl + (j // 2) % 2, 2) + lax.rem(core + j % 2, 2),
        )
        for j in range(1, 8)
    ]
    x_place = xh * 4 + xl * 2 + core

    ids = itertools.count()
    started = []

    def send(src, dst, device):
        at = next(ids)
        copy = pltpu.make_async_remote_copy(
            src_ref=src,
            dst_ref=dst,
            send_sem=send_sem.at[at],
            recv_sem=recv_sem.at[at],
            device_id=device,
            device_id_type=MESH,
        )
        copy.start()
        started.append(copy)
        return copy

    half_a = pl.ds(0, FEAT // 2)
    half_b = pl.ds(FEAT // 2, FEAT // 2)

    feat_copy = pltpu.make_async_copy(feat_hbm, feat_v, local_sem.at[0])
    feat_copy.start()
    per_chunk = SLOTS // CHUNKS
    tile_copies = [
        pltpu.make_async_copy(
            tiles_hbm.at[pl.ds(i * per_chunk, per_chunk)],
            tile_v.at[pl.ds(i * per_chunk, per_chunk)],
            tile_sem.at[i],
        )
        for i in range(CHUNKS)
    ]
    for copy in tile_copies:
        copy.start()
    up_copy = pltpu.make_async_copy(up_hbm, up_v, local_sem.at[1])
    up_copy.start()

    barrier = pltpu.get_barrier_semaphore()
    peers = y_peers + z_peers + x_peers + [k_plus, k_minus, single]
    for peer in peers:
        pl.semaphore_signal(barrier, inc=1, device_id=peer, device_id_type=MESH)

    norm = 1.0 / jnp.sqrt(deg_ref[...].astype(F32) + 1.0)
    feat_copy.wait()
    features = feat_v[...].astype(F32)
    own_x = (norm * jnp.concatenate([features[i * TS : (i + 1) * TS].T for i in range(4)], axis=1)).astype(BF)
    xblk[0] = own_x
    pl.semaphore_wait(barrier, len(peers))

    x_a = send(xblk.at[0, half_a], xtransit.at[0], x_plus)
    x_b = send(xblk.at[0, half_b], xtransit.at[1], x_minus)
    own_pa = send(xblk.at[0, half_a], xblk.at[3, half_a], y_plus)
    own_mb = send(xblk.at[0, half_b], xblk.at[1, half_b], y_minus)
    own_pb = send(xblk.at[0, half_b], xblk.at[3, half_b], y_plus)
    own_ma = send(xblk.at[0, half_a], xblk.at[1, half_a], y_minus)

    count = count_s[0]
    places = (
        lax.broadcasted_iota(jnp.int32, (8, 128), 0) * 128
        + lax.broadcasted_iota(jnp.int32, (8, 128), 1)
    )

    def add_slots(i, table):
        for u in range(8):
            t = i * 8 + u
            h = rows_s[t]
            gap = lax.rem(lax.div(h, 4) - blk + 35, 32)
            key = gap * 128 + lax.rem(h, 4) * 32 + cols_s[t]
            key = jnp.where(t < count, key, 4096)
            table = jnp.where(places == key, t, table)
        return table

    table_v[...] = lax.fori_loop(0, SLOTS // 8, add_slots, jnp.full((8, 128), SLOTS, jnp.int32))
    table_copy = pltpu.make_async_copy(table_v, table_s, local_sem.at[2])
    table_copy.start()
    tile_v[SLOTS] = jnp.zeros((TS, TS), BF)
    tile_t[SLOTS] = jnp.zeros((TS, TS), BF)

    x_a.wait_recv()
    fwd_a = send(xtransit.at[0], xblk.at[4, half_a], x_plus)
    x_b.wait_recv()
    fwd_b = send(xtransit.at[1], xblk.at[4, half_b], x_minus)
    own_pa.wait_recv()
    two_a = send(xblk.at[3, half_a], xblk.at[2, half_a], y_plus)
    own_mb.wait_recv()
    two_b = send(xblk.at[1, half_b], xblk.at[2, half_b], y_minus)

    def transpose_chunk(chunk):
        tile_copies[chunk].wait()

        def some(i, carry):
            for u in range(16):
                t = chunk * per_chunk + i * 16 + u
                tile_t[t] = tile_v[t].T
            return carry

        lax.fori_loop(0, per_chunk // 16, some, 0)

    for chunk in range(CHUNKS // 2):
        transpose_chunk(chunk)
    fwd_a.wait_recv()
    far_pa = send(xblk.at[4, half_a], xblk.at[7, half_a], y_plus)
    far_ma = send(xblk.at[4, half_a], xblk.at[5, half_a], y_minus)
    fwd_b.wait_recv()
    far_mb = send(xblk.at[4, half_b], xblk.at[5, half_b], y_minus)
    far_pb = send(xblk.at[4, half_b], xblk.at[7, half_b], y_plus)
    for chunk in range(CHUNKS // 2, CHUNKS):
        transpose_chunk(chunk)
    table_copy.wait()

    def source_block(slot):
        return lax.rem(y + slot % 4, 4) * 2 + lax.rem(xh + slot // 4, 2)

    def value_product(group, slots):
        lhs = jnp.concatenate([xblk[s] for s in slots], axis=1)
        rhs = jnp.concatenate(
            [
                jnp.concatenate(
                    [tile_t[table_s[group, a * 32 + source_block(s) * 4 + b]] for a in range(4)],
                    axis=1,
                )
                for s in slots
                for b in range(4)
            ],
            axis=0,
        )
        return jnp.dot(lhs, rhs, preferred_element_type=F32)

    own_pb.wait_recv()
    own_ma.wait_recv()
    for group in range(7):
        sums[group] = value_product(group, (0, 1, 3))
    far_pa.wait_recv()
    far2_a = send(xblk.at[7, half_a], xblk.at[6, half_a], y_plus)
    far_mb.wait_recv()
    far2_b = send(xblk.at[5, half_b], xblk.at[6, half_b], y_minus)
    two_a.wait_recv()
    two_b.wait_recv()
    for group in range(7):
        sums[group] = sums[group] + value_product(group, (2, 4))
    far_pb.wait_recv()
    far_ma.wait_recv()
    far2_a.wait_recv()
    far2_b.wait_recv()

    def last_value(offset):
        group = offset + 3
        return sums[group] + value_product(group, (5, 7, 6))

    mate_copies = []
    for i, offset in enumerate((-1 - 2 * core, 3 - 2 * core)):
        mate_out[i] = last_value(offset).astype(BF)
        mate_copies.append(send(mate_out.at[i], mate_in.at[i], mate))
    comb_out[2] = last_value(-3 + 6 * core).astype(BF)
    single_copy = send(comb_out.at[2], comb_in.at[2], single)
    minus_part = last_value(-2)
    mate_copies[0].wait_recv()
    comb_out[0] = (minus_part + mate_in[0].astype(F32)).astype(BF)
    minus_copy = send(comb_out.at[0], comb_in.at[0], k_minus)
    plus_part = last_value(2)
    mate_copies[1].wait_recv()
    comb_out[1] = (plus_part + mate_in[1].astype(F32)).astype(BF)
    plus_copy = send(comb_out.at[1], comb_in.at[1], k_plus)
    mate_out[2] = last_value(1 - 2 * core).astype(BF)
    mate_copies.append(send(mate_out.at[2], mate_in.at[2], mate))
    sums[3] = last_value(0) + xblk[0].astype(F32)

    up_copy.wait()
    mate_copies[2].wait_recv()
    total = sums[3] + mate_in[2].astype(F32)
    single_copy.wait_recv()
    total = total + comb_in[2].astype(F32)
    minus_copy.wait_recv()
    plus_copy.wait_recv()
    total = total + comb_in[0].astype(F32) + comb_in[1].astype(F32)
    aggregated = (norm * total).astype(BF)
    weight = weight_ref[...]
    pre_act = (
        lax.dot_general(aggregated, weight, (((0,), (0,)), ((), ())), preferred_element_type=F32)
        + bias_ref[...]
    )
    gate = 1.0 / (1.0 + jnp.exp(-pre_act))
    pre_grad = (
        up_v[...].astype(F32) * (gate + pre_act * gate * (1.0 - gate))
    ).astype(BF)
    gblk[3] = (
        norm * lax.dot_general(weight, pre_grad, (((1,), (1,)), ((), ())), preferred_element_type=F32)
    ).astype(BF)
    g_plus = send(gblk.at[3], gblk.at[1], k_plus)
    g_minus = send(gblk.at[3], gblk.at[5], k_minus)
    g_mate = send(gblk.at[3], gblk.at[2 + 2 * core], mate)
    g_single = send(gblk.at[3], gblk.at[6 - 6 * core], single)
    hidden_ref[...] = (pre_act * gate).astype(BF)

    local_weight = jnp.dot(aggregated, pre_grad, preferred_element_type=F32)
    local_bias = jnp.sum(pre_grad.astype(F32), axis=0, keepdims=True)
    for i in range(4):
        for u in range(8):
            row = i * 32 + (u // 2) * 8
            lanes = slice((u % 2) * 128, (u % 2) * 128 + 128)
            w_send[i, u, 0:8] = local_weight[row : row + 8, lanes]
            w_send[i, u, 8:16] = jnp.broadcast_to(local_bias[:, lanes], (8, 128))
    w_y_copies = [
        send(w_send.at[lax.rem(y + j, 4)], w_y.at[j - 1], y_peers[j - 1]) for j in range(1, 4)
    ]

    def grad_product(source, groups):
        lhs = jnp.concatenate([gblk[g] for g in groups], axis=1)
        rhs = jnp.concatenate(
            [
                jnp.concatenate(
                    [tile_v[table_s[g, a * 32 + source * 4 + b]] for b in range(4)], axis=1
                )
                for g in groups
                for a in range(4)
            ],
            axis=0,
        )
        return jnp.dot(lhs, rhs, preferred_element_type=F32)

    g_mate.wait_recv()
    for slot in range(8):
        sums[slot] = grad_product(source_block(slot), (3, 4 - 2 * core))
    g_plus.wait_recv()
    pass_plus = send(gblk.at[1], gblk.at[2 * core], mate)
    g_minus.wait_recv()
    pass_minus = send(gblk.at[5], gblk.at[4 + 2 * core], mate)
    for slot in range(8):
        sums[slot] = sums[slot] + grad_product(source_block(slot), (1, 5))
    for copy in w_y_copies:
        copy.wait_recv()
    w_z[...] = w_send[y] + w_y[0] + w_y[1] + w_y[2]
    w_z_copies = [
        send(w_z.at[lax.rem(z + j, 8)], w_zin.at[j - 1], z_peers[j - 1]) for j in range(1, 8)
    ]
    g_single.wait_recv()
    pass_plus.wait_recv()
    pass_minus.wait_recv()

    def last_grad(slot):
        rest = (2 - 2 * core, 6 - 2 * core, 6 * core)
        return sums[slot] + grad_product(source_block(slot), rest)

    def first_hop(part):
        col_out[part, 2] = last_grad(part * 4 + 2).astype(BF)
        to_plus = send(col_out.at[part, 2, half_a], col_mid.at[part, 0], y_plus)
        to_minus = send(col_out.at[part, 2, half_b], col_mid.at[part, 1], y_minus)
        return to_plus, to_minus

    def direct_hop(part):
        plus_value = last_grad(part * 4 + 1)
        col_out[part, 1, FEAT // 2 :] = plus_value[FEAT // 2 :].astype(BF)
        plus_b = send(col_out.at[part, 1, half_b], col_in.at[part, 0, half_b], y_plus)
        minus_value = last_grad(part * 4 + 3)
        col_out[part, 3, : FEAT // 2] = minus_value[: FEAT // 2].astype(BF)
        minus_a = send(col_out.at[part, 3, half_a], col_in.at[part, 1, half_a], y_minus)
        sums[part * 4 + 1, : FEAT // 2] = plus_value[: FEAT // 2]
        sums[part * 4 + 3, FEAT // 2 :] = minus_value[FEAT // 2 :]
        return plus_b, minus_a

    def relay_hop(part, to_plus, to_minus):
        to_plus.wait_recv()
        col_out[part, 1, : FEAT // 2] = (
            sums[part * 4 + 1, : FEAT // 2] + col_mid[part, 0].astype(F32)
        ).astype(BF)
        plus_a = send(col_out.at[part, 1, half_a], col_in.at[part, 0, half_a], y_plus)
        to_minus.wait_recv()
        col_out[part, 3, FEAT // 2 :] = (
            sums[part * 4 + 3, FEAT // 2 :] + col_mid[part, 1].astype(F32)
        ).astype(BF)
        minus_b = send(col_out.at[part, 3, half_b], col_in.at[part, 1, half_b], y_minus)
        return plus_a, minus_b

    far_first = first_hop(1)
    far_direct = direct_hop(1)
    far_relay = relay_hop(1, *far_first)
    near_first = first_hop(0)
    sums[4] = last_grad(4)
    near_direct = direct_hop(0)
    near_relay = relay_hop(0, *near_first)
    sums[0] = last_grad(0) + gblk[3].astype(F32)

    for copy in w_z_copies:
        copy.wait_recv()
    w_sum = w_z[z]
    for j in range(7):
        w_sum = w_sum + w_zin[j]
    w_x[...] = w_sum
    w_xall[x_place] = w_sum
    w_x_copies = [send(w_x, w_xall.at[x_place], x_peers[j - 1]) for j in range(1, 8)]

    for copy in far_direct + far_relay:
        copy.wait_recv()
    xsum[...] = (sums[4] + col_in[1, 0].astype(F32) + col_in[1, 1].astype(F32)).astype(BF)
    xs_a = send(xsum.at[half_a], xsum_transit.at[0], x_plus)
    xs_b = send(xsum.at[half_b], xsum_transit.at[1], x_minus)

    for copy in w_x_copies:
        copy.wait_recv()
    w_sum = w_xall[0]
    for j in range(1, 8):
        w_sum = w_sum + w_xall[j]
    w_x_total = w_sum
    w_zall[z] = w_x_total
    w_zin_out = w_all.at[4, 0]
    w_all[4, 0] = w_x_total
    w_g_copies = [send(w_zin_out, w_zall.at[z], z_peers[j - 1]) for j in range(1, 8)]

    xs_a.wait_recv()
    xt_a = send(xsum_transit.at[0], xsum_in.at[half_a], x_plus)
    xs_b.wait_recv()
    xt_b = send(xsum_transit.at[1], xsum_in.at[half_b], x_minus)
    for copy in near_direct + near_relay:
        copy.wait_recv()
    column = sums[0] + col_in[0, 0].astype(F32) + col_in[0, 1].astype(F32)
    for copy in w_g_copies:
        copy.wait_recv()
    w_all[y] = w_zall[...]
    w_f_copies = [send(w_zall, w_all.at[y], y_peers[j - 1]) for j in range(1, 4)]
    xt_a.wait_recv()
    xt_b.wait_recv()
    feature_grad = norm * (column + xsum_in[...].astype(F32))
    for i in range(4):
        fgrad_ref[i * TS : (i + 1) * TS, :] = feature_grad[:, i * TS : (i + 1) * TS].T.astype(BF)
    scale = NODES ** (-0.5)
    for copy in w_f_copies:
        copy.wait_recv()
    bgrad_ref[:, 0:128] = w_all[0, 0, 8:9] * scale
    bgrad_ref[:, 128:256] = w_all[0, 1, 8:9] * scale
    for i in range(4):
        for u in range(8):
            row = i * 32 + (u // 2) * 8
            lane = (u % 2) * 128
            wgrad_ref[row : row + 8, lane : lane + 128] = w_all[i, u, 0:8] * scale
    for copy in started:
        copy.wait_send()


def on_device(
    features, degrees, tile_weights, tile_rows, tile_cols, tile_counts, weight, layer_bias, upstream
):
    vmem = pl.BlockSpec(memory_space=pltpu.VMEM)
    smem = pl.BlockSpec(memory_space=pltpu.SMEM)
    anywhere = pl.BlockSpec(memory_space=pl.ANY)
    blocks = lambda *lead: pltpu.VMEM((*lead, FEAT, ROWS), BF)
    halves = lambda *lead: pltpu.VMEM((*lead, FEAT // 2, ROWS), BF)
    units = lambda *lead: pltpu.VMEM((*lead, 16, 128), F32)
    hidden, feature_grad, weight_grad, bias_grad = pl.pallas_call(
        kernel,
        in_specs=[smem, smem, smem, anywhere, vmem, anywhere, vmem, vmem, anywhere],
        out_specs=[vmem, vmem, vmem, vmem],
        out_shape=[
            jax.ShapeDtypeStruct((ROWS, HID), BF),
            jax.ShapeDtypeStruct((ROWS, FEAT), BF),
            jax.ShapeDtypeStruct((FEAT, HID), F32),
            jax.ShapeDtypeStruct((1, HID), F32),
        ],
        scratch_shapes=[
            pltpu.VMEM((ROWS, FEAT), BF),
            pltpu.VMEM((ROWS, HID), BF),
            pltpu.VMEM((SLOTS + 1, TS, TS), BF),
            pltpu.VMEM((SLOTS + 1, TS, TS), BF),
            pltpu.VMEM((8, FEAT, ROWS), F32),
            blocks(8),
            halves(2),
            blocks(3),
            blocks(3),
            blocks(3),
            blocks(3),
            blocks(7),
            blocks(2, 4),
            halves(2, 2),
            blocks(2, 2),
            blocks(),
            halves(2),
            blocks(),
            units(4, 8),
            units(3, 8),
            units(8),
            units(7),
            units(),
            units(8),
            units(8),
            units(5, 8),
            pltpu.VMEM((8, 128), jnp.int32),
            pltpu.SMEM((8, 128), jnp.int32),
            pltpu.SemaphoreType.DMA((3,)),
            pltpu.SemaphoreType.DMA((CHUNKS,)),
            pltpu.SemaphoreType.DMA((N_COPIES,)),
            pltpu.SemaphoreType.DMA((N_COPIES,)),
        ],
        compiler_params=pltpu.CompilerParams(
            collective_id=0, has_side_effects=True, vmem_limit_bytes=56 << 20
        ),
        name="layer",
    )(
        tile_rows.reshape(SLOTS),
        tile_cols.reshape(SLOTS),
        tile_counts.reshape(1),
        features,
        degrees.reshape(1, ROWS),
        tile_weights.reshape(SLOTS, TS, TS),
        weight,
        layer_bias.reshape(1, HID),
        upstream,
    )
    return hidden, feature_grad, weight_grad, bias_grad.reshape(HID)


def solution(mesh):
    placed = (
        P(("rep", "blk"), None),
        P(("rep", "blk")),
        P("rep", "blk", None, None, None),
        P("rep", "blk", None),
        P("rep", "blk", None),
        P("rep", "blk"),
        P(),
        P(),
        P(("rep", "blk"), None),
    )
    return jax.shard_map(
        on_device,
        mesh=mesh,
        in_specs=placed,
        out_specs=(P(("rep", "blk"), None), P(("rep", "blk"), None), P(), P()),
        check_vma=False,
    )
```

time: 561 us -> 80.1 us (0.14)
  waiting for transfers between devices: 189 us -> 0 us
  other arithmetic: 164 us -> 2.55 us
  blocking collectives: 75.9 us -> 0 us
  Pallas kernels: 0 us -> 69.2 us
  matrix products: 55.7 us -> 0 us
  local copies, waits for them, and re-layouts: 42.9 us -> 6.05 us
  starting transfers between devices: 14.4 us -> 0 us
  between operations: 14.6 us -> 1.29 us
    scatter-add x16 -> x0, other arithmetic: 105 us -> none  [add_block(): jax.ops.segment_sum(products, segment_part, segment_total + 1)]
    reduce_scatter x1 -> x0, waiting for transfers between devices: 77.9 us -> none  [on_device(): lax.psum_scatter(column_part.reshape(rep_count * row_count, feat_width).a...]
    psum x1 -> x0, blocking collectives: 75.9 us -> none  [on_device(): weight_sum, bias_sum = lax.psum((local_weight, local_bias), ('rep', 'blk'))]
    pallas_call x0 -> x1, Pallas kernels: none -> 69.2 us  [on_device(): pl.pallas_call(kernel, in_specs=[smem, smem, smem, anywhere, vmem, anywhe...]
    dot_general x19 -> x0, matrix products: 55.7 us -> none  [the longest x16 53.5 us: add_block(): jnp.einsum(pattern, weights_part, source_tiles[gather_part], preferred_el...]
    all_gather x1 -> x0, waiting for transfers between devices: 53.4 us -> none  [on_device(): source_rows = lax.all_gather(scaled, 'rep', axis=0, tiled=True)]
    add x16 -> x0, other arithmetic: 46.3 us -> none  [add_block(): running + jax.ops.segment_sum(products, segment_part, segment_total + 1)[...]
    psum x1 -> x0, waiting for transfers between devices: 41.2 us -> none  [on_device(): weight_sum, bias_sum = lax.psum((local_weight, local_bias), ('rep', 'blk'))]
  transfers between devices with their start and end apart: 15 -> 0, of which waited for: 7 -> 0; matrix products, arithmetic and copies ran while one was open for 24% -> 0% of each run, Pallas kernels for 0% -> 0%
where the time goes in v1:
time: 80.1 us; the launch traced here: 79.1 us
  Pallas kernels  69.2 us (86%)
  local copies, waits for them, and re-layouts  6.05 us (8%)
  other arithmetic  2.55 us (3%)
  between operations  1.29 us (2%)
    pallas_call x1, Pallas kernels, on_device(): pl.pallas_call(kernel, in_specs=[smem, smem, smem, anywhere, vmem, anywhe...  69.2 us
    unnamed x4, local copies, waits for them, and re-layouts  6.05 us
    unnamed x2, other arithmetic  2.55 us

profile of v1, /device:TPU:32, one launch (start us, length us, event | category | flops | bytes accessed | tf_op | source)
XLA Modules:
  0.0 79.1 jit_solution(2263921506958526480)
XLA Ops:
  1.3 1.3 %reduce.rows_s = s32[320]{0:T(512)} reduce(s32[1,1,320]{2,1,0:T(1,128)} %param.12, s32[]{:T(128)} %constant.4), dimensions={0,1}, to_apply=%param.12.reduce_sub_computation | reduce | bytes 2564 | tf_op args[3]
  2.6 1.3 %reduce.1.cols_s = s32[320]{0:T(512)} reduce(s32[1,1,320]{2,1,0:T(1,128)} %param.13, s32[]{:T(128)} %constant.4), dimensions={0,1}, to_apply=%param.13.reduce_sub_computation | reduce | bytes 2564 | tf_op args[4]
  3.8 69.2 %layer.1 = (bf16[512,256]{1,0:T(8,128)(2,1)}, bf16[512,128]{1,0:T(8,128)(2,1)}, f32[128,256]{1,0:T(8,128)}, f32[1,256]{1,0:T(1,128)}) custom-call(s32[320]{0:T(512)} %reduce.rows_s, s32[320]{0:T(512)} %reduce.1.cols_s, s32[1]{0:T(128)} %bitcast.5.count_s, bf16[512,128]{1,0:T(8,128)(2,1)} %feat_hbm.1, s32[1,512]{1,0:T(1,128)} %bitcast.7, ...), custom_call_target="tpu_custom_call" | custom-call | tf_op jit(solution)/shard_map/layer/pallas_call | solution.py:443
  73.0 1.7 %copy.18 = bf16[512,256]{1,0:T(8,128)(2,1)} copy(bf16[512,256]{1,0:T(8,128)(2,1)} %get-tuple-element.16) | data formatting | bytes 524288
  74.7 1.6 %copy.19 = bf16[512,128]{1,0:T(8,128)(2,1)} copy(bf16[512,128]{1,0:T(8,128)(2,1)} %get-tuple-element.17) | data formatting | bytes 262144
  76.2 1.6 %copy.20 = f32[128,256]{1,0:T(8,128)} copy(f32[128,256]{1,0:T(8,128)} %get-tuple-element.18) | data formatting | bytes 262144
  77.8 1.2 %copy.21 = f32[256]{0:T(256)} copy(f32[256]{0:T(256)} %bitcast.9) | data formatting | bytes 2048

commit v2 on v1

--- a/solution.py
+++ b/solution.py
@@ -15,7 +15,8 @@
 ROWS = 512
 FEAT = 128
 HID = 256
-N_COPIES = 80
+QUARTER = 32
+N_COPIES = 128
 CHUNKS = 10
 NODES = 131072
 
@@ -23,7 +24,7 @@
 def kernel(
     rows_s,
     cols_s,
-    count_s,
+    count_hbm,
     feat_hbm,
     deg_ref,
     tiles_hbm,
@@ -58,10 +59,12 @@
     w_zin,
     w_x,
     w_xall,
+    w_x_total,
     w_zall,
     w_all,
     table_v,
     table_s,
+    count_s,
     local_sem,
     tile_sem,
     send_sem,
@@ -111,11 +114,20 @@
         started.append(copy)
         return copy
 
-    half_a = pl.ds(0, FEAT // 2)
-    half_b = pl.ds(FEAT // 2, FEAT // 2)
+    low = [pl.ds(i * QUARTER, QUARTER) for i in range(2)]
+    high = [pl.ds(FEAT // 2 + i * QUARTER, QUARTER) for i in range(2)]
+
+    def send_parts(src, dst, parts, device):
+        return [send(src.at[part], dst.at[part], device) for part in parts]
+
+    def arrived(copies):
+        for copy in copies:
+            copy.wait_recv()
 
     feat_copy = pltpu.make_async_copy(feat_hbm, feat_v, local_sem.at[0])
     feat_copy.start()
+    count_copy = pltpu.make_async_copy(count_hbm, count_s, local_sem.at[3])
+    count_copy.start()
     per_chunk = SLOTS // CHUNKS
     tile_copies = [
         pltpu.make_async_copy(
@@ -142,14 +154,19 @@
     xblk[0] = own_x
     pl.semaphore_wait(barrier, len(peers))
 
-    x_a = send(xblk.at[0, half_a], xtransit.at[0], x_plus)
-    x_b = send(xblk.at[0, half_b], xtransit.at[1], x_minus)
-    own_pa = send(xblk.at[0, half_a], xblk.at[3, half_a], y_plus)
-    own_mb = send(xblk.at[0, half_b], xblk.at[1, half_b], y_minus)
-    own_pb = send(xblk.at[0, half_b], xblk.at[3, half_b], y_plus)
-    own_ma = send(xblk.at[0, half_a], xblk.at[1, half_a], y_minus)
-
-    count = count_s[0]
+    own = xblk.at[0]
+    x_a = [send(own.at[low[i]], xtransit.at[0, i], x_plus) for i in range(2)]
+    x_b = [send(own.at[high[i]], xtransit.at[1, i], x_minus) for i in range(2)]
+    own_pa, own_mb, own_pb, own_ma = [], [], [], []
+    for i in range(2):
+        own_pa.append(send(own.at[low[i]], xblk.at[3, low[i]], y_plus))
+        own_mb.append(send(own.at[high[i]], xblk.at[1, high[i]], y_minus))
+    for i in range(2):
+        own_pb.append(send(own.at[high[i]], xblk.at[3, high[i]], y_plus))
+        own_ma.append(send(own.at[low[i]], xblk.at[1, low[i]], y_minus))
+
+    count_copy.wait()
+    count = count_s[0, 0]
     places = (
         lax.broadcasted_iota(jnp.int32, (8, 128), 0) * 128
         + lax.broadcasted_iota(jnp.int32, (8, 128), 1)
@@ -158,9 +175,9 @@
     def add_slots(i, table):
         for u in range(8):
             t = i * 8 + u
-            h = rows_s[t]
+            h = rows_s[0, 0, t]
             gap = lax.rem(lax.div(h, 4) - blk + 35, 32)
-            key = gap * 128 + lax.rem(h, 4) * 32 + cols_s[t]
+            key = gap * 128 + lax.rem(h, 4) * 32 + cols_s[0, 0, t]
             key = jnp.where(t < count, key, 4096)
             table = jnp.where(places == key, t, table)
         return table
@@ -171,14 +188,16 @@
     tile_v[SLOTS] = jnp.zeros((TS, TS), BF)
     tile_t[SLOTS] = jnp.zeros((TS, TS), BF)
 
-    x_a.wait_recv()
-    fwd_a = send(xtransit.at[0], xblk.at[4, half_a], x_plus)
-    x_b.wait_recv()
-    fwd_b = send(xtransit.at[1], xblk.at[4, half_b], x_minus)
-    own_pa.wait_recv()
-    two_a = send(xblk.at[3, half_a], xblk.at[2, half_a], y_plus)
-    own_mb.wait_recv()
-    two_b = send(xblk.at[1, half_b], xblk.at[2, half_b], y_minus)
+    fwd_a, fwd_b, two_a, two_b = [], [], [], []
+    for i in range(2):
+        x_a[i].wait_recv()
+        fwd_a.append(send(xtransit.at[0, i], xblk.at[4, low[i]], x_plus))
+        x_b[i].wait_recv()
+        fwd_b.append(send(xtransit.at[1, i], xblk.at[4, high[i]], x_minus))
+        own_pa[i].wait_recv()
+        two_a.append(send(xblk.at[3, low[i]], xblk.at[2, low[i]], y_plus))
+        own_mb[i].wait_recv()
+        two_b.append(send(xblk.at[1, high[i]], xblk.at[2, high[i]], y_minus))
 
     def transpose_chunk(chunk):
         tile_copies[chunk].wait()
@@ -191,16 +210,24 @@
 
         lax.fori_loop(0, per_chunk // 16, some, 0)
 
-    for chunk in range(CHUNKS // 2):
+    for chunk in range(4):
         transpose_chunk(chunk)
-    fwd_a.wait_recv()
-    far_pa = send(xblk.at[4, half_a], xblk.at[7, half_a], y_plus)
-    far_ma = send(xblk.at[4, half_a], xblk.at[5, half_a], y_minus)
-    fwd_b.wait_recv()
-    far_mb = send(xblk.at[4, half_b], xblk.at[5, half_b], y_minus)
-    far_pb = send(xblk.at[4, half_b], xblk.at[7, half_b], y_plus)
-    for chunk in range(CHUNKS // 2, CHUNKS):
+    far_pa, far_ma, far_pb, far_mb = [], [], [], []
+    for i in range(2):
+        fwd_a[i].wait_recv()
+        far_pa.append(send(xblk.at[4, low[i]], xblk.at[7, low[i]], y_plus))
+        fwd_b[i].wait_recv()
+        far_mb.append(send(xblk.at[4, high[i]], xblk.at[5, high[i]], y_minus))
+        far_ma.append(send(xblk.at[4, low[i]], xblk.at[5, low[i]], y_minus))
+        far_pb.append(send(xblk.at[4, high[i]], xblk.at[7, high[i]], y_plus))
+    for chunk in range(4, CHUNKS):
         transpose_chunk(chunk)
+    far2_a, far2_b = [], []
+    for i in range(2):
+        far_pa[i].wait_recv()
+        far2_a.append(send(xblk.at[7, low[i]], xblk.at[6, low[i]], y_plus))
+        far_mb[i].wait_recv()
+        far2_b.append(send(xblk.at[5, high[i]], xblk.at[6, high[i]], y_minus))
     table_copy.wait()
 
     def source_block(slot):
@@ -221,26 +248,17 @@
         )
         return jnp.dot(lhs, rhs, preferred_element_type=F32)
 
-    own_pb.wait_recv()
-    own_ma.wait_recv()
+    arrived(own_pb + own_ma)
     for group in range(7):
         sums[group] = value_product(group, (0, 1, 3))
-    far_pa.wait_recv()
-    far2_a = send(xblk.at[7, half_a], xblk.at[6, half_a], y_plus)
-    far_mb.wait_recv()
-    far2_b = send(xblk.at[5, half_b], xblk.at[6, half_b], y_minus)
-    two_a.wait_recv()
-    two_b.wait_recv()
+    arrived(two_a + two_b + far_pb + far_ma)
     for group in range(7):
-        sums[group] = sums[group] + value_product(group, (2, 4))
-    far_pb.wait_recv()
-    far_ma.wait_recv()
-    far2_a.wait_recv()
-    far2_b.wait_recv()
+        sums[group] = sums[group] + value_product(group, (2, 4, 5, 7))
+    arrived(far2_a + far2_b)
 
     def last_value(offset):
         group = offset + 3
-        return sums[group] + value_product(group, (5, 7, 6))
+        return sums[group] + value_product(group, (6,))
 
     mate_copies = []
     for i, offset in enumerate((-1 - 2 * core, 3 - 2 * core)):
@@ -296,8 +314,9 @@
             w_send[i, u, 0:8] = local_weight[row : row + 8, lanes]
             w_send[i, u, 8:16] = jnp.broadcast_to(local_bias[:, lanes], (8, 128))
     w_y_copies = [
-        send(w_send.at[lax.rem(y + j, 4)], w_y.at[j - 1], y_peers[j - 1]) for j in range(1, 4)
+        send(w_send.at[lax.rem(y + j, 4)], w_y.at[y], y_peers[j - 1]) for j in range(1, 4)
     ]
+    w_y[y] = w_send[y]
 
     def grad_product(source, groups):
         lhs = jnp.concatenate([gblk[g] for g in groups], axis=1)
@@ -320,17 +339,14 @@
     pass_plus = send(gblk.at[1], gblk.at[2 * core], mate)
     g_minus.wait_recv()
     pass_minus = send(gblk.at[5], gblk.at[4 + 2 * core], mate)
-    for slot in range(8):
-        sums[slot] = sums[slot] + grad_product(source_block(slot), (1, 5))
-    for copy in w_y_copies:
-        copy.wait_recv()
-    w_z[...] = w_send[y] + w_y[0] + w_y[1] + w_y[2]
+    arrived(w_y_copies)
+    w_z[...] = w_y[0] + w_y[1] + w_y[2] + w_y[3]
     w_z_copies = [
         send(w_z.at[lax.rem(z + j, 8)], w_zin.at[j - 1], z_peers[j - 1]) for j in range(1, 8)
     ]
-    g_single.wait_recv()
-    pass_plus.wait_recv()
-    pass_minus.wait_recv()
+    for slot in range(8):
+        sums[slot] = sums[slot] + grad_product(source_block(slot), (1, 5))
+    arrived([g_single, pass_plus, pass_minus])
 
     def last_grad(slot):
         rest = (2 - 2 * core, 6 - 2 * core, 6 * core)
@@ -338,97 +354,111 @@
 
     def first_hop(part):
         col_out[part, 2] = last_grad(part * 4 + 2).astype(BF)
-        to_plus = send(col_out.at[part, 2, half_a], col_mid.at[part, 0], y_plus)
-        to_minus = send(col_out.at[part, 2, half_b], col_mid.at[part, 1], y_minus)
+        source = col_out.at[part, 2]
+        to_plus = [send(source.at[low[i]], col_mid.at[part, 0, i], y_plus) for i in range(2)]
+        to_minus = [send(source.at[high[i]], col_mid.at[part, 1, i], y_minus) for i in range(2)]
         return to_plus, to_minus
 
     def direct_hop(part):
-        plus_value = last_grad(part * 4 + 1)
-        col_out[part, 1, FEAT // 2 :] = plus_value[FEAT // 2 :].astype(BF)
-        plus_b = send(col_out.at[part, 1, half_b], col_in.at[part, 0, half_b], y_plus)
-        minus_value = last_grad(part * 4 + 3)
-        col_out[part, 3, : FEAT // 2] = minus_value[: FEAT // 2].astype(BF)
-        minus_a = send(col_out.at[part, 3, half_a], col_in.at[part, 1, half_a], y_minus)
-        sums[part * 4 + 1, : FEAT // 2] = plus_value[: FEAT // 2]
-        sums[part * 4 + 3, FEAT // 2 :] = minus_value[FEAT // 2 :]
+        col_out[part, 1, FEAT // 2 :] = sums[part * 4 + 1, FEAT // 2 :].astype(BF)
+        plus_b = send_parts(col_out.at[part, 1], col_in.at[part, 0], high, y_plus)
+        col_out[part, 3, : FEAT // 2] = sums[part * 4 + 3, : FEAT // 2].astype(BF)
+        minus_a = send_parts(col_out.at[part, 3], col_in.at[part, 1], low, y_minus)
         return plus_b, minus_a
 
     def relay_hop(part, to_plus, to_minus):
-        to_plus.wait_recv()
-        col_out[part, 1, : FEAT // 2] = (
-            sums[part * 4 + 1, : FEAT // 2] + col_mid[part, 0].astype(F32)
-        ).astype(BF)
-        plus_a = send(col_out.at[part, 1, half_a], col_in.at[part, 0, half_a], y_plus)
-        to_minus.wait_recv()
-        col_out[part, 3, FEAT // 2 :] = (
-            sums[part * 4 + 3, FEAT // 2 :] + col_mid[part, 1].astype(F32)
-        ).astype(BF)
-        minus_b = send(col_out.at[part, 3, half_b], col_in.at[part, 1, half_b], y_minus)
+        plus_a, minus_b = [], []
+        for i in range(2):
+            to_plus[i].wait_recv()
+            col_out[part, 1, low[i]] = (
+                sums[part * 4 + 1, low[i]] + col_mid[part, 0, i].astype(F32)
+            ).astype(BF)
+            plus_a.append(
+                send(col_out.at[part, 1, low[i]], col_in.at[part, 0, low[i]], y_plus)
+            )
+            to_minus[i].wait_recv()
+            col_out[part, 3, high[i]] = (
+                sums[part * 4 + 3, high[i]] + col_mid[part, 1, i].astype(F32)
+            ).astype(BF)
+            minus_b.append(
+                send(col_out.at[part, 3, high[i]], col_in.at[part, 1, high[i]], y_minus)
+            )
         return plus_a, minus_b
 
     far_first = first_hop(1)
-    far_direct = direct_hop(1)
-    far_relay = relay_hop(1, *far_first)
-    near_first = first_hop(0)
-    sums[4] = last_grad(4)
-    near_direct = direct_hop(0)
-    near_relay = relay_hop(0, *near_first)
-    sums[0] = last_grad(0) + gblk[3].astype(F32)
-
-    for copy in w_z_copies:
-        copy.wait_recv()
+    for slot in (5, 7):
+        sums[slot] = last_grad(slot)
+    far_plus_b, far_minus_a = direct_hop(1)
+    for slot in (4, 1, 3):
+        sums[slot] = last_grad(slot)
+    arrived(w_z_copies)
     w_sum = w_z[z]
     for j in range(7):
         w_sum = w_sum + w_zin[j]
     w_x[...] = w_sum
     w_xall[x_place] = w_sum
     w_x_copies = [send(w_x, w_xall.at[x_place], x_peers[j - 1]) for j in range(1, 8)]
-
-    for copy in far_direct + far_relay:
-        copy.wait_recv()
-    xsum[...] = (sums[4] + col_in[1, 0].astype(F32) + col_in[1, 1].astype(F32)).astype(BF)
-    xs_a = send(xsum.at[half_a], xsum_transit.at[0], x_plus)
-    xs_b = send(xsum.at[half_b], xsum_transit.at[1], x_minus)
-
-    for copy in w_x_copies:
-        copy.wait_recv()
+    far_plus_a, far_minus_b = relay_hop(1, *far_first)
+    near_first = first_hop(0)
+    near_plus_b, near_minus_a = direct_hop(0)
+    sums[0] = last_grad(0) + gblk[3].astype(F32)
+
+    arrived(w_x_copies)
     w_sum = w_xall[0]
     for j in range(1, 8):
         w_sum = w_sum + w_xall[j]
-    w_x_total = w_sum
-    w_zall[z] = w_x_total
-    w_zin_out = w_all.at[4, 0]
-    w_all[4, 0] = w_x_total
-    w_g_copies = [send(w_zin_out, w_zall.at[z], z_peers[j - 1]) for j in range(1, 8)]
-
-    xs_a.wait_recv()
-    xt_a = send(xsum_transit.at[0], xsum_in.at[half_a], x_plus)
-    xs_b.wait_recv()
-    xt_b = send(xsum_transit.at[1], xsum_in.at[half_b], x_minus)
-    for copy in near_direct + near_relay:
-        copy.wait_recv()
+    w_x_total[...] = w_sum
+    w_zall[z] = w_sum
+    w_g_copies = [send(w_x_total, w_zall.at[z], z_peers[j - 1]) for j in range(1, 8)]
+
+    def partner_sum(part):
+        xsum[part] = (
+            sums[4, part] + col_in[1, 0, part].astype(F32) + col_in[1, 1, part].astype(F32)
+        ).astype(BF)
+
+    arrived(far_plus_b + far_minus_a)
+    xs_a, xs_b = [], []
+    for i in range(2):
+        far_plus_a[i].wait_recv()
+        partner_sum(low[i])
+        xs_a.append(send(xsum.at[low[i]], xsum_transit.at[0, i], x_plus))
+        far_minus_b[i].wait_recv()
+        partner_sum(high[i])
+        xs_b.append(send(xsum.at[high[i]], xsum_transit.at[1, i], x_minus))
+    near_plus_a, near_minus_b = relay_hop(0, *near_first)
+    xt_a, xt_b = [], []
+    for i in range(2):
+        xs_a[i].wait_recv()
+        xt_a.append(send(xsum_transit.at[0, i], xsum_in.at[low[i]], x_plus))
+        xs_b[i].wait_recv()
+        xt_b.append(send(xsum_transit.at[1, i], xsum_in.at[high[i]], x_minus))
+    arrived(w_g_copies)
+    w_f_copies = [
+        send(w_zall.at[:, pl.ds(0, 8)], w_all.at[y], y_peers[j - 1]) for j in range(1, 4)
+    ]
+    w_all[y] = w_zall[:, 0:8]
+    scale = NODES ** (-0.5)
+    bgrad_ref[:, 0:128] = w_zall[0, 8:9] * scale
+    bgrad_ref[:, 128:256] = w_zall[1, 8:9] * scale
+    arrived(near_plus_b + near_minus_a + near_plus_a + near_minus_b)
     column = sums[0] + col_in[0, 0].astype(F32) + col_in[0, 1].astype(F32)
-    for copy in w_g_copies:
-        copy.wait_recv()
-    w_all[y] = w_zall[...]
-    w_f_copies = [send(w_zall, w_all.at[y], y_peers[j - 1]) for j in range(1, 4)]
-    xt_a.wait_recv()
-    xt_b.wait_recv()
-    feature_grad = norm * (column + xsum_in[...].astype(F32))
-    for i in range(4):
-        fgrad_ref[i * TS : (i + 1) * TS, :] = feature_grad[:, i * TS : (i + 1) * TS].T.astype(BF)
-    scale = NODES ** (-0.5)
-    for copy in w_f_copies:
-        copy.wait_recv()
-    bgrad_ref[:, 0:128] = w_all[0, 0, 8:9] * scale
-    bgrad_ref[:, 128:256] = w_all[0, 1, 8:9] * scale
+    arrived(w_f_copies)
     for i in range(4):
         for u in range(8):
             row = i * 32 + (u // 2) * 8
             lane = (u % 2) * 128
-            wgrad_ref[row : row + 8, lane : lane + 128] = w_all[i, u, 0:8] * scale
+            wgrad_ref[row : row + 8, lane : lane + 128] = w_all[i, u] * scale
+    arrived(xt_a + xt_b)
+    feature_grad = norm * (column + xsum_in[...].astype(F32))
+    for i in range(4):
+        fgrad_ref[i * TS : (i + 1) * TS, :] = feature_grad[:, i * TS : (i + 1) * TS].T.astype(BF)
     for copy in started:
         copy.wait_send()
+
+
+def settle(*refs):
+    for source, target in zip(refs[:4], refs[4:]):
+        target[...] = source[...]
 
 
 def on_device(
@@ -438,18 +468,19 @@
     smem = pl.BlockSpec(memory_space=pltpu.SMEM)
     anywhere = pl.BlockSpec(memory_space=pl.ANY)
     blocks = lambda *lead: pltpu.VMEM((*lead, FEAT, ROWS), BF)
-    halves = lambda *lead: pltpu.VMEM((*lead, FEAT // 2, ROWS), BF)
+    quarters = lambda *lead: pltpu.VMEM((*lead, QUARTER, ROWS), BF)
     units = lambda *lead: pltpu.VMEM((*lead, 16, 128), F32)
-    hidden, feature_grad, weight_grad, bias_grad = pl.pallas_call(
+    shapes = [
+        jax.ShapeDtypeStruct((ROWS, HID), BF),
+        jax.ShapeDtypeStruct((ROWS, FEAT), BF),
+        jax.ShapeDtypeStruct((FEAT, HID), F32),
+        jax.ShapeDtypeStruct((1, HID), F32),
+    ]
+    results = pl.pallas_call(
         kernel,
-        in_specs=[smem, smem, smem, anywhere, vmem, anywhere, vmem, vmem, anywhere],
+        in_specs=[smem, smem, anywhere, anywhere, vmem, anywhere, vmem, vmem, anywhere],
         out_specs=[vmem, vmem, vmem, vmem],
-        out_shape=[
-            jax.ShapeDtypeStruct((ROWS, HID), BF),
-            jax.ShapeDtypeStruct((ROWS, FEAT), BF),
-            jax.ShapeDtypeStruct((FEAT, HID), F32),
-            jax.ShapeDtypeStruct((1, HID), F32),
-        ],
+        out_shape=shapes,
         scratch_shapes=[
             pltpu.VMEM((ROWS, FEAT), BF),
             pltpu.VMEM((ROWS, HID), BF),
@@ -457,29 +488,31 @@
             pltpu.VMEM((SLOTS + 1, TS, TS), BF),
             pltpu.VMEM((8, FEAT, ROWS), F32),
             blocks(8),
-            halves(2),
+            quarters(2, 2),
             blocks(3),
             blocks(3),
             blocks(3),
             blocks(3),
             blocks(7),
             blocks(2, 4),
-            halves(2, 2),
+            quarters(2, 2, 2),
             blocks(2, 2),
             blocks(),
-            halves(2),
+            quarters(2, 2),
             blocks(),
             units(4, 8),
-            units(3, 8),
+            units(4, 8),
             units(8),
             units(7),
             units(),
             units(8),
+            units(),
             units(8),
-            units(5, 8),
+            pltpu.VMEM((4, 8, 8, 128), F32),
             pltpu.VMEM((8, 128), jnp.int32),
             pltpu.SMEM((8, 128), jnp.int32),
-            pltpu.SemaphoreType.DMA((3,)),
+            pltpu.SMEM((1, 1), jnp.int32),
+            pltpu.SemaphoreType.DMA((4,)),
             pltpu.SemaphoreType.DMA((CHUNKS,)),
             pltpu.SemaphoreType.DMA((N_COPIES,)),
             pltpu.SemaphoreType.DMA((N_COPIES,)),
@@ -489,9 +522,9 @@
         ),
         name="layer",
     )(
-        tile_rows.reshape(SLOTS),
-        tile_cols.reshape(SLOTS),
-        tile_counts.reshape(1),
+        tile_rows,
+        tile_cols,
+        tile_counts,
         features,
         degrees.reshape(1, ROWS),
         tile_weights.reshape(SLOTS, TS, TS),
@@ -499,6 +532,9 @@
         layer_bias.reshape(1, HID),
         upstream,
     )
+    hidden, feature_grad, weight_grad, bias_grad = pl.pallas_call(
+        settle, in_specs=[vmem] * 4, out_specs=[vmem] * 4, out_shape=shapes, name="settle"
+    )(*results)
     return hidden, feature_grad, weight_grad, bias_grad.reshape(HID)
 
 

time: 80.1 us -> 66.9 us (0.84)
  local copies, waits for them, and re-layouts: 6.05 us -> 0 us
  Pallas kernels: 69.2 us -> 64.6 us
  other arithmetic: 2.55 us -> 0 us
    unnamed x4 -> x0, local copies, waits for them, and re-layouts: 6.05 us -> none
    pallas_call x1 -> x2, Pallas kernels: 69.2 us -> 64.6 us  [the longest x1 62.7 us: on_device(): pl.pallas_call(kernel, in_specs=[smem, smem, anywhere, anywhere, vmem, an...]
    unnamed x2 -> x0, other arithmetic: 2.55 us -> none
where the time goes in v2:
time: 66.9 us; the launch traced here: 65.9 us
  Pallas kernels  64.6 us (97%)
  between operations  1.29 us (2%)
    pallas_call x1, Pallas kernels, on_device(): pl.pallas_call(kernel, in_specs=[smem, smem, anywhere, anywhere, vmem, an...  62.7 us
    pallas_call x1, Pallas kernels, on_device(): pl.pallas_call(settle, in_specs=[vmem] * 4, out_specs=[vmem] * 4, out_sha...  1.85 us

profile of v2, /device:TPU:32, one launch (start us, length us, event | category | flops | bytes accessed | tf_op | source)
XLA Modules:
  0.0 65.9 jit_solution(9557219595313962140)
XLA Ops:
  1.3 62.7 %layer.1 = (bf16[512,256]{1,0:T(8,128)(2,1)}, bf16[512,128]{1,0:T(8,128)(2,1)}, f32[128,256]{1,0:T(8,128)}, f32[1,256]{1,0:T(1,128)}) custom-call(s32[1,1,320]{2,1,0:T(1,128)} %rows_s.1, s32[1,1,320]{2,1,0:T(1,128)} %cols_s.1, s32[1,1]{1,0:T(1,128)S(6)} %copy.13.count_hbm, bf16[512,128]{1,0:T(8,128)(2,1)} %feat_hbm.1, s32[1,512]{1,0:T(1,128)} %bitcast.5, ...), custom_call_target="tpu_custom_call" | custom-call | tf_op jit(solution)/shard_map/layer/pallas_call | solution.py:479
  64.0 1.8 %settle.1 = (bf16[512,256]{1,0:T(8,128)(2,1)}, bf16[512,128]{1,0:T(8,128)(2,1)}, f32[128,256]{1,0:T(8,128)}, f32[1,256]{1,0:T(1,128)}) custom-call(bf16[512,256]{1,0:T(8,128)(2,1)} %get-tuple-element.12.refs_0_, bf16[512,128]{1,0:T(8,128)(2,1)} %get-tuple-element.13.refs_1_, f32[128,256]{1,0:T(8,128)} %get-tuple-element.14.refs_2_, ...), custom_call_target="tpu_custom_call" | custom-call | tf_op jit(solution)/shard_map/settle/pallas_call | solution.py:535

commit v3 on v2

--- a/solution.py
+++ b/solution.py
@@ -13,6 +13,7 @@
 SLOTS = 320
 TS = 128
 ROWS = 512
+HALF = 256
 FEAT = 128
 HID = 256
 QUARTER = 32
@@ -251,62 +252,88 @@
     arrived(own_pb + own_ma)
     for group in range(7):
         sums[group] = value_product(group, (0, 1, 3))
-    arrived(two_a + two_b + far_pb + far_ma)
+    arrived(two_a + two_b)
     for group in range(7):
-        sums[group] = sums[group] + value_product(group, (2, 4, 5, 7))
+        sums[group] = sums[group] + value_product(group, (2, 4))
+    arrived(far_pb + far_ma)
+    for group in range(7):
+        sums[group] = sums[group] + value_product(group, (5, 7))
     arrived(far2_a + far2_b)
 
     def last_value(offset):
         group = offset + 3
         return sums[group] + value_product(group, (6,))
 
-    mate_copies = []
+    columns = [slice(h * HALF, (h + 1) * HALF) for h in range(2)]
+    mate_copies = [[], [], []]
     for i, offset in enumerate((-1 - 2 * core, 3 - 2 * core)):
-        mate_out[i] = last_value(offset).astype(BF)
-        mate_copies.append(send(mate_out.at[i], mate_in.at[i], mate))
-    comb_out[2] = last_value(-3 + 6 * core).astype(BF)
-    single_copy = send(comb_out.at[2], comb_in.at[2], single)
-    minus_part = last_value(-2)
-    mate_copies[0].wait_recv()
-    comb_out[0] = (minus_part + mate_in[0].astype(F32)).astype(BF)
-    minus_copy = send(comb_out.at[0], comb_in.at[0], k_minus)
-    plus_part = last_value(2)
-    mate_copies[1].wait_recv()
-    comb_out[1] = (plus_part + mate_in[1].astype(F32)).astype(BF)
-    plus_copy = send(comb_out.at[1], comb_in.at[1], k_plus)
-    mate_out[2] = last_value(1 - 2 * core).astype(BF)
-    mate_copies.append(send(mate_out.at[2], mate_in.at[2], mate))
+        value = last_value(offset).astype(BF)
+        for h in range(2):
+            mate_out[i, h] = value[:, columns[h]]
+        mate_copies[i].append(send(mate_out.at[i, 0], mate_in.at[i, 0], mate))
+    for i in range(2):
+        mate_copies[i].append(send(mate_out.at[i, 1], mate_in.at[i, 1], mate))
+    value = last_value(-3 + 6 * core).astype(BF)
+    single_copies = []
+    for h in range(2):
+        comb_out[2, h] = value[:, columns[h]]
+        single_copies.append(send(comb_out.at[2, h], comb_in.at[2, h], single))
+    for offset in (-2, 2):
+        sums[offset + 3] = last_value(offset)
+    minus_copies, plus_copies = [], []
+    for h in range(2):
+        mate_copies[0][h].wait_recv()
+        comb_out[0, h] = (sums[1, :, columns[h]] + mate_in[0, h].astype(F32)).astype(BF)
+        minus_copies.append(send(comb_out.at[0, h], comb_in.at[0, h], k_minus))
+        mate_copies[1][h].wait_recv()
+        comb_out[1, h] = (sums[5, :, columns[h]] + mate_in[1, h].astype(F32)).astype(BF)
+        plus_copies.append(send(comb_out.at[1, h], comb_in.at[1, h], k_plus))
+        if h == 0:
+            value = last_value(1 - 2 * core).astype(BF)
+            for part in range(2):
+                mate_out[2, part] = value[:, columns[part]]
+                mate_copies[2].append(send(mate_out.at[2, part], mate_in.at[2, part], mate))
     sums[3] = last_value(0) + xblk[0].astype(F32)
 
     up_copy.wait()
-    mate_copies[2].wait_recv()
-    total = sums[3] + mate_in[2].astype(F32)
-    single_copy.wait_recv()
-    total = total + comb_in[2].astype(F32)
-    minus_copy.wait_recv()
-    plus_copy.wait_recv()
-    total = total + comb_in[0].astype(F32) + comb_in[1].astype(F32)
-    aggregated = (norm * total).astype(BF)
     weight = weight_ref[...]
-    pre_act = (
-        lax.dot_general(aggregated, weight, (((0,), (0,)), ((), ())), preferred_element_type=F32)
-        + bias_ref[...]
-    )
-    gate = 1.0 / (1.0 + jnp.exp(-pre_act))
-    pre_grad = (
-        up_v[...].astype(F32) * (gate + pre_act * gate * (1.0 - gate))
-    ).astype(BF)
-    gblk[3] = (
-        norm * lax.dot_general(weight, pre_grad, (((1,), (1,)), ((), ())), preferred_element_type=F32)
-    ).astype(BF)
-    g_plus = send(gblk.at[3], gblk.at[1], k_plus)
-    g_minus = send(gblk.at[3], gblk.at[5], k_minus)
-    g_mate = send(gblk.at[3], gblk.at[2 + 2 * core], mate)
-    g_single = send(gblk.at[3], gblk.at[6 - 6 * core], single)
-    hidden_ref[...] = (pre_act * gate).astype(BF)
-
-    local_weight = jnp.dot(aggregated, pre_grad, preferred_element_type=F32)
-    local_bias = jnp.sum(pre_grad.astype(F32), axis=0, keepdims=True)
+    g_plus, g_minus, g_mate, g_single = [], [], [], []
+    kept = []
+    for h in range(2):
+        norm_h = norm[:, columns[h]]
+        mate_copies[2][h].wait_recv()
+        single_copies[h].wait_recv()
+        total = sums[3, :, columns[h]] + mate_in[2, h].astype(F32) + comb_in[2, h].astype(F32)
+        minus_copies[h].wait_recv()
+        plus_copies[h].wait_recv()
+        total = total + comb_in[0, h].astype(F32) + comb_in[1, h].astype(F32)
+        aggregated = (norm_h * total).astype(BF)
+        pre_act = (
+            lax.dot_general(
+                aggregated, weight, (((0,), (0,)), ((), ())), preferred_element_type=F32
+            )
+            + bias_ref[...]
+        )
+        gate = 1.0 / (1.0 + jnp.exp(-pre_act))
+        rows = slice(h * HALF, (h + 1) * HALF)
+        pre_grad = (
+            up_v[rows, :].astype(F32) * (gate + pre_act * gate * (1.0 - gate))
+        ).astype(BF)
+        gblk[3, h] = (
+            norm_h
+            * lax.dot_general(
+                weight, pre_grad, (((1,), (1,)), ((), ())), preferred_element_type=F32
+            )
+        ).astype(BF)
+        g_plus.append(send(gblk.at[3, h], gblk.at[1, h], k_plus))
+        g_minus.append(send(gblk.at[3, h], gblk.at[5, h], k_minus))
+        g_mate.append(send(gblk.at[3, h], gblk.at[2 + 2 * core, h], mate))
+        g_single.append(send(gblk.at[3, h], gblk.at[6 - 6 * core, h], single))
+        hidden_ref[rows, :] = (pre_act * gate).astype(BF)
+        kept.append((aggregated, pre_grad))
+
+    local_weight = sum(jnp.dot(a, p, preferred_element_type=F32) for a, p in kept)
+    local_bias = sum(jnp.sum(p.astype(F32), axis=0, keepdims=True) for _, p in kept)
     for i in range(4):
         for u in range(8):
             row = i * 32 + (u // 2) * 8
@@ -319,7 +346,7 @@
     w_y[y] = w_send[y]
 
     def grad_product(source, groups):
-        lhs = jnp.concatenate([gblk[g] for g in groups], axis=1)
+        lhs = jnp.concatenate([gblk[g, h] for g in groups for h in range(2)], axis=1)
         rhs = jnp.concatenate(
             [
                 jnp.concatenate(
@@ -332,13 +359,15 @@
         )
         return jnp.dot(lhs, rhs, preferred_element_type=F32)
 
-    g_mate.wait_recv()
+    arrived(g_mate)
     for slot in range(8):
         sums[slot] = grad_product(source_block(slot), (3, 4 - 2 * core))
-    g_plus.wait_recv()
-    pass_plus = send(gblk.at[1], gblk.at[2 * core], mate)
-    g_minus.wait_recv()
-    pass_minus = send(gblk.at[5], gblk.at[4 + 2 * core], mate)
+    passed = []
+    for h in range(2):
+        g_plus[h].wait_recv()
+        passed.append(send(gblk.at[1, h], gblk.at[2 * core, h], mate))
+        g_minus[h].wait_recv()
+        passed.append(send(gblk.at[5, h], gblk.at[4 + 2 * core, h], mate))
     arrived(w_y_copies)
     w_z[...] = w_y[0] + w_y[1] + w_y[2] + w_y[3]
     w_z_copies = [
@@ -346,7 +375,7 @@
     ]
     for slot in range(8):
         sums[slot] = sums[slot] + grad_product(source_block(slot), (1, 5))
-    arrived([g_single, pass_plus, pass_minus])
+    arrived(g_single + passed)
 
     def last_grad(slot):
         rest = (2 - 2 * core, 6 - 2 * core, 6 * core)
@@ -401,7 +430,8 @@
     far_plus_a, far_minus_b = relay_hop(1, *far_first)
     near_first = first_hop(0)
     near_plus_b, near_minus_a = direct_hop(0)
-    sums[0] = last_grad(0) + gblk[3].astype(F32)
+    own_grad = jnp.concatenate([gblk[3, 0], gblk[3, 1]], axis=1)
+    sums[0] = last_grad(0) + own_grad.astype(F32)
 
     arrived(w_x_copies)
     w_sum = w_xall[0]
@@ -468,6 +498,7 @@
     smem = pl.BlockSpec(memory_space=pltpu.SMEM)
     anywhere = pl.BlockSpec(memory_space=pl.ANY)
     blocks = lambda *lead: pltpu.VMEM((*lead, FEAT, ROWS), BF)
+    parts = lambda *lead: pltpu.VMEM((*lead, 2, FEAT, HALF), BF)
     quarters = lambda *lead: pltpu.VMEM((*lead, QUARTER, ROWS), BF)
     units = lambda *lead: pltpu.VMEM((*lead, 16, 128), F32)
     shapes = [
@@ -489,11 +520,11 @@
             pltpu.VMEM((8, FEAT, ROWS), F32),
             blocks(8),
             quarters(2, 2),
-            blocks(3),
-            blocks(3),
-            blocks(3),
-            blocks(3),
-            blocks(7),
+            parts(3),
+            parts(3),
+            parts(3),
+            parts(3),
+            parts(7),
             blocks(2, 4),
             quarters(2, 2, 2),
             blocks(2, 2),

time: 66.9 us -> 66.6 us (level); the launches traced: 65.9 us -> 66.5 us
  no operation moved by 1% of the time
where the time goes in v3:
time: 66.6 us; the launch traced here: 66.5 us
  Pallas kernels  65.2 us (98%)
  between operations  1.29 us (2%)
    pallas_call x1, Pallas kernels, on_device(): pl.pallas_call(kernel, in_specs=[smem, smem, anywhere, anywhere, vmem, an...  63.3 us
    pallas_call x1, Pallas kernels, on_device(): pl.pallas_call(settle, in_specs=[vmem] * 4, out_specs=[vmem] * 4, out_sha...  1.85 us

profile of v3, /device:TPU:32, one launch (start us, length us, event | category | flops | bytes accessed | tf_op | source)
XLA Modules:
  0.0 66.5 jit_solution(14199482579918587102)
XLA Ops:
  1.3 63.3 %layer.1 = (bf16[512,256]{1,0:T(8,128)(2,1)}, bf16[512,128]{1,0:T(8,128)(2,1)}, f32[128,256]{1,0:T(8,128)}, f32[1,256]{1,0:T(1,128)}) custom-call(s32[1,1,320]{2,1,0:T(1,128)} %rows_s.1, s32[1,1,320]{2,1,0:T(1,128)} %cols_s.1, s32[1,1]{1,0:T(1,128)S(6)} %copy.13.count_hbm, bf16[512,128]{1,0:T(8,128)(2,1)} %feat_hbm.1, s32[1,512]{1,0:T(1,128)} %bitcast.5, ...), custom_call_target="tpu_custom_call" | custom-call | tf_op jit(solution)/shard_map/layer/pallas_call | solution.py:510
  64.6 1.8 %settle.1 = (bf16[512,256]{1,0:T(8,128)(2,1)}, bf16[512,128]{1,0:T(8,128)(2,1)}, f32[128,256]{1,0:T(8,128)}, f32[1,256]{1,0:T(1,128)}) custom-call(bf16[512,256]{1,0:T(8,128)(2,1)} %get-tuple-element.12.refs_0_, bf16[512,128]{1,0:T(8,128)(2,1)} %get-tuple-element.13.refs_1_, f32[128,256]{1,0:T(8,128)} %get-tuple-element.14.refs_2_, ...), custom_call_target="tpu_custom_call" | custom-call | tf_op jit(solution)/shard_map/settle/pallas_call | solution.py:566

commit v4 on v3

--- a/solution.py
+++ b/solution.py
@@ -42,7 +42,6 @@
     tile_t,
     sums,
     xblk,
-    xtransit,
     mate_out,
     mate_in,
     comb_out,
@@ -52,7 +51,6 @@
     col_mid,
     col_in,
     xsum,
-    xsum_transit,
     xsum_in,
     w_send,
     w_y,
@@ -80,9 +78,7 @@
     core = lax.rem(blk, 2)
     y_plus = (lax.rem(rep + 2, 8), blk)
     y_minus = (lax.rem(rep + 6, 8), blk)
-    blk_x = blk + 2 - 4 * xl
-    x_plus = (2 * y + lax.rem(xh + xl, 2), blk_x)
-    x_minus = (2 * y + lax.rem(xh + 1 - xl, 2), blk_x)
+    partner = (2 * y + 1 - xh, blk)
     mate = (rep, blk + 1 - 2 * core)
     k_plus = (rep, lax.rem(blk + 2, 32))
     k_minus = (rep, lax.rem(blk + 30, 32))
@@ -156,8 +152,10 @@
     pl.semaphore_wait(barrier, len(peers))
 
     own = xblk.at[0]
-    x_a = [send(own.at[low[i]], xtransit.at[0, i], x_plus) for i in range(2)]
-    x_b = [send(own.at[high[i]], xtransit.at[1, i], x_minus) for i in range(2)]
+    far_a, far_b = [], []
+    for i in range(2):
+        far_a.append(send(own.at[low[i]], xblk.at[4, low[i]], partner))
+        far_b.append(send(own.at[high[i]], xblk.at[4, high[i]], partner))
     own_pa, own_mb, own_pb, own_ma = [], [], [], []
     for i in range(2):
         own_pa.append(send(own.at[low[i]], xblk.at[3, low[i]], y_plus))
@@ -177,8 +175,8 @@
         for u in range(8):
             t = i * 8 + u
             h = rows_s[0, 0, t]
-            gap = lax.rem(lax.div(h, 4) - blk + 35, 32)
-            key = gap * 128 + lax.rem(h, 4) * 32 + cols_s[0, 0, t]
+            gap = (lax.shift_right_logical(h, 2) - blk + 35) & 31
+            key = (gap << 7) + ((h & 3) << 5) + cols_s[0, 0, t]
             key = jnp.where(t < count, key, 4096)
             table = jnp.where(places == key, t, table)
         return table
@@ -189,17 +187,6 @@
     tile_v[SLOTS] = jnp.zeros((TS, TS), BF)
     tile_t[SLOTS] = jnp.zeros((TS, TS), BF)
 
-    fwd_a, fwd_b, two_a, two_b = [], [], [], []
-    for i in range(2):
-        x_a[i].wait_recv()
-        fwd_a.append(send(xtransit.at[0, i], xblk.at[4, low[i]], x_plus))
-        x_b[i].wait_recv()
-        fwd_b.append(send(xtransit.at[1, i], xblk.at[4, high[i]], x_minus))
-        own_pa[i].wait_recv()
-        two_a.append(send(xblk.at[3, low[i]], xblk.at[2, low[i]], y_plus))
-        own_mb[i].wait_recv()
-        two_b.append(send(xblk.at[1, high[i]], xblk.at[2, high[i]], y_minus))
-
     def transpose_chunk(chunk):
         tile_copies[chunk].wait()
 
@@ -211,17 +198,28 @@
 
         lax.fori_loop(0, per_chunk // 16, some, 0)
 
-    for chunk in range(4):
+    for chunk in range(2):
+        transpose_chunk(chunk)
+    two_a, two_b = [], []
+    for i in range(2):
+        own_pa[i].wait_recv()
+        two_a.append(send(xblk.at[3, low[i]], xblk.at[2, low[i]], y_plus))
+        own_mb[i].wait_recv()
+        two_b.append(send(xblk.at[1, high[i]], xblk.at[2, high[i]], y_minus))
+    for chunk in range(2, 4):
         transpose_chunk(chunk)
     far_pa, far_ma, far_pb, far_mb = [], [], [], []
     for i in range(2):
-        fwd_a[i].wait_recv()
+        far_a[i].wait_recv()
         far_pa.append(send(xblk.at[4, low[i]], xblk.at[7, low[i]], y_plus))
-        fwd_b[i].wait_recv()
+        far_b[i].wait_recv()
         far_mb.append(send(xblk.at[4, high[i]], xblk.at[5, high[i]], y_minus))
         far_ma.append(send(xblk.at[4, low[i]], xblk.at[5, low[i]], y_minus))
         far_pb.append(send(xblk.at[4, high[i]], xblk.at[7, high[i]], y_plus))
-    for chunk in range(4, CHUNKS):
+        if i == 0:
+            for chunk in range(4, 6):
+                transpose_chunk(chunk)
+    for chunk in range(6, CHUNKS):
         transpose_chunk(chunk)
     far2_a, far2_b = [], []
     for i in range(2):
@@ -451,17 +449,11 @@
     for i in range(2):
         far_plus_a[i].wait_recv()
         partner_sum(low[i])
-        xs_a.append(send(xsum.at[low[i]], xsum_transit.at[0, i], x_plus))
+        xs_a.append(send(xsum.at[low[i]], xsum_in.at[low[i]], partner))
         far_minus_b[i].wait_recv()
         partner_sum(high[i])
-        xs_b.append(send(xsum.at[high[i]], xsum_transit.at[1, i], x_minus))
+        xs_b.append(send(xsum.at[high[i]], xsum_in.at[high[i]], partner))
     near_plus_a, near_minus_b = relay_hop(0, *near_first)
-    xt_a, xt_b = [], []
-    for i in range(2):
-        xs_a[i].wait_recv()
-        xt_a.append(send(xsum_transit.at[0, i], xsum_in.at[low[i]], x_plus))
-        xs_b[i].wait_recv()
-        xt_b.append(send(xsum_transit.at[1, i], xsum_in.at[high[i]], x_minus))
     arrived(w_g_copies)
     w_f_copies = [
         send(w_zall.at[:, pl.ds(0, 8)], w_all.at[y], y_peers[j - 1]) for j in range(1, 4)
@@ -478,7 +470,7 @@
             row = i * 32 + (u // 2) * 8
             lane = (u % 2) * 128
             wgrad_ref[row : row + 8, lane : lane + 128] = w_all[i, u] * scale
-    arrived(xt_a + xt_b)
+    arrived(xs_a + xs_b)
     feature_grad = norm * (column + xsum_in[...].astype(F32))
     for i in range(4):
         fgrad_ref[i * TS : (i + 1) * TS, :] = feature_grad[:, i * TS : (i + 1) * TS].T.astype(BF)
@@ -519,7 +511,6 @@
             pltpu.VMEM((SLOTS + 1, TS, TS), BF),
             pltpu.VMEM((8, FEAT, ROWS), F32),
             blocks(8),
-            quarters(2, 2),
             parts(3),
             parts(3),
             parts(3),
@@ -529,7 +520,6 @@
             quarters(2, 2, 2),
             blocks(2, 2),
             blocks(),
-            quarters(2, 2),
             blocks(),
             units(4, 8),
             units(4, 8),

time: 66.6 us -> 62.8 us (0.943)
  Pallas kernels: 65.2 us -> 61.2 us
    pallas_call x1, Pallas kernels: 63.3 us -> 59.3 us  [on_device(): pl.pallas_call(kernel, in_specs=[smem, smem, anywhere, anywhere, vmem, an...]
where the time goes in v4:
time: 62.8 us; the launch traced here: 62.5 us
  Pallas kernels  61.2 us (97%)
  between operations  1.29 us (2%)
    pallas_call x1, Pallas kernels, on_device(): pl.pallas_call(kernel, in_specs=[smem, smem, anywhere, anywhere, vmem, an...  59.3 us
    pallas_call x1, Pallas kernels, on_device(): pl.pallas_call(settle, in_specs=[vmem] * 4, out_specs=[vmem] * 4, out_sha...  1.85 us

profile of v4, /device:TPU:32, one launch (start us, length us, event | category | flops | bytes accessed | tf_op | source)
XLA Modules:
  0.0 62.5 jit_solution(2759581493375066088)
XLA Ops:
  1.3 59.3 %layer.1 = (bf16[512,256]{1,0:T(8,128)(2,1)}, bf16[512,128]{1,0:T(8,128)(2,1)}, f32[128,256]{1,0:T(8,128)}, f32[1,256]{1,0:T(1,128)}) custom-call(s32[1,1,320]{2,1,0:T(1,128)} %rows_s.1, s32[1,1,320]{2,1,0:T(1,128)} %cols_s.1, s32[1,1]{1,0:T(1,128)S(6)} %copy.13.count_hbm, bf16[512,128]{1,0:T(8,128)(2,1)} %feat_hbm.1, s32[1,512]{1,0:T(1,128)} %bitcast.5, ...), custom_call_target="tpu_custom_call" | custom-call | tf_op jit(solution)/shard_map/layer/pallas_call | solution.py:502
  60.6 1.8 %settle.1 = (bf16[512,256]{1,0:T(8,128)(2,1)}, bf16[512,128]{1,0:T(8,128)(2,1)}, f32[128,256]{1,0:T(8,128)}, f32[1,256]{1,0:T(1,128)}) custom-call(bf16[512,256]{1,0:T(8,128)(2,1)} %get-tuple-element.12.refs_0_, bf16[512,128]{1,0:T(8,128)(2,1)} %get-tuple-element.13.refs_1_, f32[128,256]{1,0:T(8,128)} %get-tuple-element.14.refs_2_, ...), custom_call_target="tpu_custom_call" | custom-call | tf_op jit(solution)/shard_map/settle/pallas_call | solution.py:556

commit v5 on v4

--- a/solution.py
+++ b/solution.py
@@ -32,10 +32,11 @@
     weight_ref,
     bias_ref,
     up_hbm,
-    hidden_ref,
+    hidden_hbm,
     fgrad_ref,
     wgrad_ref,
     bgrad_ref,
+    hidden_v,
     feat_v,
     up_v,
     tile_v,
@@ -121,6 +122,11 @@
         for copy in copies:
             copy.wait_recv()
 
+    barrier = pltpu.get_barrier_semaphore()
+    peers = z_peers + y_peers + x_peers + [k_plus, k_minus, single]
+    for peer in peers:
+        pl.semaphore_signal(barrier, inc=1, device_id=peer, device_id_type=MESH)
+
     feat_copy = pltpu.make_async_copy(feat_hbm, feat_v, local_sem.at[0])
     feat_copy.start()
     count_copy = pltpu.make_async_copy(count_hbm, count_s, local_sem.at[3])
@@ -138,11 +144,6 @@
         copy.start()
     up_copy = pltpu.make_async_copy(up_hbm, up_v, local_sem.at[1])
     up_copy.start()
-
-    barrier = pltpu.get_barrier_semaphore()
-    peers = y_peers + z_peers + x_peers + [k_plus, k_minus, single]
-    for peer in peers:
-        pl.semaphore_signal(barrier, inc=1, device_id=peer, device_id_type=MESH)
 
     norm = 1.0 / jnp.sqrt(deg_ref[...].astype(F32) + 1.0)
     feat_copy.wait()
@@ -327,9 +328,11 @@
         g_minus.append(send(gblk.at[3, h], gblk.at[5, h], k_minus))
         g_mate.append(send(gblk.at[3, h], gblk.at[2 + 2 * core, h], mate))
         g_single.append(send(gblk.at[3, h], gblk.at[6 - 6 * core, h], single))
-        hidden_ref[rows, :] = (pre_act * gate).astype(BF)
+        hidden_v[rows, :] = (pre_act * gate).astype(BF)
         kept.append((aggregated, pre_grad))
 
+    hidden_copy = pltpu.make_async_copy(hidden_v, hidden_hbm, local_sem.at[4])
+    hidden_copy.start()
     local_weight = sum(jnp.dot(a, p, preferred_element_type=F32) for a, p in kept)
     local_bias = sum(jnp.sum(p.astype(F32), axis=0, keepdims=True) for _, p in kept)
     for i in range(4):
@@ -360,17 +363,17 @@
     arrived(g_mate)
     for slot in range(8):
         sums[slot] = grad_product(source_block(slot), (3, 4 - 2 * core))
+    arrived(w_y_copies)
+    w_z[...] = w_y[0] + w_y[1] + w_y[2] + w_y[3]
+    w_z_copies = [
+        send(w_z.at[lax.rem(z + j, 8)], w_zin.at[j - 1], z_peers[j - 1]) for j in range(1, 8)
+    ]
     passed = []
     for h in range(2):
         g_plus[h].wait_recv()
         passed.append(send(gblk.at[1, h], gblk.at[2 * core, h], mate))
         g_minus[h].wait_recv()
         passed.append(send(gblk.at[5, h], gblk.at[4 + 2 * core, h], mate))
-    arrived(w_y_copies)
-    w_z[...] = w_y[0] + w_y[1] + w_y[2] + w_y[3]
-    w_z_copies = [
-        send(w_z.at[lax.rem(z + j, 8)], w_zin.at[j - 1], z_peers[j - 1]) for j in range(1, 8)
-    ]
     for slot in range(8):
         sums[slot] = sums[slot] + grad_product(source_block(slot), (1, 5))
     arrived(g_single + passed)
@@ -474,13 +477,22 @@
     feature_grad = norm * (column + xsum_in[...].astype(F32))
     for i in range(4):
         fgrad_ref[i * TS : (i + 1) * TS, :] = feature_grad[:, i * TS : (i + 1) * TS].T.astype(BF)
+    hidden_copy.wait()
     for copy in started:
         copy.wait_send()
 
 
 def settle(*refs):
-    for source, target in zip(refs[:4], refs[4:]):
-        target[...] = source[...]
+    in_sem, out_sem = refs[12:]
+    loads = [pltpu.make_async_copy(refs[i], refs[8 + i], in_sem.at[i]) for i in range(4)]
+    stores = [pltpu.make_async_copy(refs[8 + i], refs[4 + i], out_sem.at[i]) for i in range(4)]
+    for load in loads:
+        load.start()
+    for load, store in zip(loads, stores):
+        load.wait()
+        store.start()
+    for store in stores:
+        store.wait()
 
 
 def on_device(
@@ -502,9 +514,10 @@
     results = pl.pallas_call(
         kernel,
         in_specs=[smem, smem, anywhere, anywhere, vmem, anywhere, vmem, vmem, anywhere],
-        out_specs=[vmem, vmem, vmem, vmem],
+        out_specs=[anywhere, vmem, vmem, vmem],
         out_shape=shapes,
         scratch_shapes=[
+            pltpu.VMEM((ROWS, HID), BF),
             pltpu.VMEM((ROWS, FEAT), BF),
             pltpu.VMEM((ROWS, HID), BF),
             pltpu.VMEM((SLOTS + 1, TS, TS), BF),
@@ -533,7 +546,7 @@
             pltpu.VMEM((8, 128), jnp.int32),
             pltpu.SMEM((8, 128), jnp.int32),
             pltpu.SMEM((1, 1), jnp.int32),
-            pltpu.SemaphoreType.DMA((4,)),
+            pltpu.SemaphoreType.DMA((5,)),
             pltpu.SemaphoreType.DMA((CHUNKS,)),
             pltpu.SemaphoreType.DMA((N_COPIES,)),
             pltpu.SemaphoreType.DMA((N_COPIES,)),
@@ -554,7 +567,13 @@
         upstream,
     )
     hidden, feature_grad, weight_grad, bias_grad = pl.pallas_call(
-        settle, in_specs=[vmem] * 4, out_specs=[vmem] * 4, out_shape=shapes, name="settle"
+        settle,
+        in_specs=[anywhere] * 4,
+        out_specs=[anywhere] * 4,
+        out_shape=shapes,
+        scratch_shapes=[pltpu.VMEM(shape.shape, shape.dtype) for shape in shapes]
+        + [pltpu.SemaphoreType.DMA((4,)), pltpu.SemaphoreType.DMA((4,))],
+        name="settle",
     )(*results)
     return hidden, feature_grad, weight_grad, bias_grad.reshape(HID)
 

time: 62.8 us -> 63.2 us (level); the launches traced: 62.5 us -> 62.2 us
  no operation moved by 1% of the time
where the time goes in v5:
time: 63.2 us; the launch traced here: 62.2 us
  Pallas kernels  60.7 us (96%)
  between operations  1.45 us (2%)
    pallas_call x1, Pallas kernels, on_device(): pl.pallas_call(kernel, in_specs=[smem, smem, anywhere, anywhere, vmem, an...  58.9 us
    pallas_call x1, Pallas kernels, on_device(): pl.pallas_call(settle, in_specs=[anywhere] * 4, out_specs=[anywhere] * 4,...  1.81 us

profile of v5, /device:TPU:32, one launch (start us, length us, event | category | flops | bytes accessed | tf_op | source)
XLA Modules:
  0.0 62.2 jit_solution(7468308956725988727)
XLA Ops:
  1.3 58.9 %layer.1 = (bf16[512,256]{1,0:T(8,128)(2,1)}, bf16[512,128]{1,0:T(8,128)(2,1)}, f32[128,256]{1,0:T(8,128)}, f32[1,256]{1,0:T(1,128)}) custom-call(s32[1,1,320]{2,1,0:T(1,128)} %rows_s.1, s32[1,1,320]{2,1,0:T(1,128)} %cols_s.1, s32[1,1]{1,0:T(1,128)S(6)} %copy.13.count_hbm, bf16[512,128]{1,0:T(8,128)(2,1)} %feat_hbm.1, s32[1,512]{1,0:T(1,128)} %bitcast.5, ...), custom_call_target="tpu_custom_call" | custom-call | tf_op jit(solution)/shard_map/layer/pallas_call | solution.py:514
  60.2 1.8 %settle.1 = (bf16[512,256]{1,0:T(8,128)(2,1)}, bf16[512,128]{1,0:T(8,128)(2,1)}, f32[128,256]{1,0:T(8,128)}, f32[1,256]{1,0:T(1,128)}) custom-call(bf16[512,256]{1,0:T(8,128)(2,1)} %get-tuple-element.12.refs_0_, bf16[512,128]{1,0:T(8,128)(2,1)} %get-tuple-element.13.refs_1_, f32[128,256]{1,0:T(8,128)} %get-tuple-element.14.refs_2_, ...), custom_call_target="tpu_custom_call" | custom-call | tf_op jit(solution)/shard_map/settle/pallas_call | solution.py:569
